TPU v7x, 32 devices: a whole 2x2x4 slice. The times are simulated.
32 devices in a mesh: gx: 2 (over x), gy: 8 (over z, y), cp: 2 (over core).
Axes of the slice: x: 2, y: 2, z: 4, core: 2. Of those that a mesh axis runs over, the one named last changes fastest.
Arguments:
- start_vectors: float32 [8, 8, 192, 256], P(None, None, 'gy', 'gx'), may hold values from -6 to 6
- potential: float32 [8, 192, 256], P(None, 'gy', 'gx'), may hold values from -1.1 to 1.1
Outputs:
- filtered_basis: float32 [8, 8, 192, 256], P(None, None, 'gy', 'gx')
- projected: float32 [8, 8], replicated
All inputs are finite; a program needn't handle non-finite values.
Results may differ from a plain program's by a relative error of at most 0.0003.
Values sent between devices are 32-bit elements; how exact they have to be, the bound alone decides.
No kernel may reach another device: no remote copies, remote signals or barrier semaphores. Data moves between devices by JAX's collectives and lax.ppermute only.
A program may use at most 64 MiB of HBM per device.

v0:
```python
import math

import jax
import jax.numpy as jnp
from jax import lax
from jax.sharding import PartitionSpec as P

POINTS = 4
ITERS = 3


diag_shift = 3.0
kinetic_half = 0.5
contour_centre = -1.0
contour_radius = 2.0


def with_halo(block, sides, width):
    for axis, dim in sides:
        count = lax.axis_size(axis)
        forward = [(i, i + 1) for i in range(count - 1)]
        forward.append((count - 1, 0))
        backward = [(target, source) for source, target in forward]
        low = lax.ppermute(
            lax.slice_in_dim(block, block.shape[dim] - width, None, axis=dim), axis, forward
        )
        high = lax.ppermute(lax.slice_in_dim(block, 0, width, axis=dim), axis, backward)
        block = jnp.concatenate([low, block, high], axis=dim)
    return block


def contour(index):
    angle = math.pi * (jnp.asarray(index).astype(jnp.float32) + 0.5) / POINTS
    shift_real = contour_centre + contour_radius * jnp.cos(angle)
    shift_imag = contour_radius * jnp.sin(angle)
    weight_real = contour_radius / POINTS * jnp.cos(angle)
    weight_imag = contour_radius / POINTS * jnp.sin(angle)
    return (shift_real, shift_imag, weight_real, weight_imag)


def apply_hamiltonian(widened, potential):
    centre = widened[..., 1:-1, 1:-1]
    near = widened[..., :-2, 1:-1] + widened[..., 2:, 1:-1]
    near = near + widened[..., 1:-1, :-2] + widened[..., 1:-1, 2:]
    zeros = jnp.zeros_like(centre[..., :1, :, :])
    near = (
        near
        + jnp.concatenate([zeros, centre[..., :-1, :, :]], axis=-3)
        + jnp.concatenate([centre[..., 1:, :, :], zeros], axis=-3)
    )
    return (diag_shift + potential) * centre - kinetic_half * near


def trim_rows(array, margin):
    return array[..., margin : array.shape[-2] - margin, :]


def point_tables(first_point, local_count, diagonal):
    indices = first_point + jnp.arange(local_count, dtype=jnp.int32)
    shift_real, shift_imag, weight_real, weight_imag = contour(indices)
    shaped = [
        value.reshape(local_count, 1, 1, 1, 1)
        for value in (shift_real, shift_imag, weight_real, weight_imag)
    ]
    offset = shaped[0] - diagonal[None, None]
    magnitude = offset * offset + shaped[1] * shaped[1]
    inverse_real = offset / magnitude
    inverse_imag = -shaped[1] / magnitude
    return (shaped[0], shaped[1], shaped[2], shaped[3], inverse_real, inverse_imag)


def jacobi_update(
    real_part,
    imag_part,
    image_real,
    image_imag,
    vectors,
    shift_real,
    shift_imag,
    inverse_real,
    inverse_imag,
):
    resid_real = vectors - (shift_real * real_part - shift_imag * imag_part - image_real)
    resid_imag = -(shift_real * imag_part + shift_imag * real_part - image_imag)
    return (
        real_part + (inverse_real * resid_real - inverse_imag * resid_imag),
        imag_part + (inverse_real * resid_imag + inverse_imag * resid_real),
    )


def per_device(start_vectors, potential):
    local_count = POINTS // lax.axis_size("cp")
    first_point = lax.axis_index("cp") * local_count
    joined = jnp.concatenate([start_vectors, potential[None]], axis=0)
    widened = with_halo(joined, (("gy", 2),), ITERS)
    vectors_wide = widened[:-1]
    potential_wide = widened[-1]
    shift_real, shift_imag, weight_real, weight_imag, inverse_real, inverse_imag = point_tables(
        first_point, local_count, diag_shift + potential_wide
    )
    real_part = inverse_real * vectors_wide[None]
    imag_part = inverse_imag * vectors_wide[None]
    for iteration in range(1, ITERS):
        padded = with_halo(jnp.concatenate([real_part, imag_part], axis=0), (("gx", 4),), 1)
        images = apply_hamiltonian(padded, trim_rows(potential_wide, iteration))
        real_part, imag_part = jacobi_update(
            trim_rows(real_part, 1),
            trim_rows(imag_part, 1),
            images[:local_count],
            images[local_count:],
            trim_rows(vectors_wide, iteration),
            shift_real,
            shift_imag,
            trim_rows(inverse_real, iteration),
            trim_rows(inverse_imag, iteration),
        )
    running = jnp.sum(weight_real * real_part - weight_imag * imag_part, axis=0)
    summed = lax.psum(running, "cp")
    padded_sum = with_halo(summed, (("gx", 3),), 1)
    image = apply_hamiltonian(padded_sum, potential)
    filtered = trim_rows(summed, 1)
    vectors_count = filtered.shape[0]
    flat = filtered.reshape(vectors_count, -1)
    image_flat = image.reshape(vectors_count, -1)
    gram_part = jnp.dot(
        flat, flat.T, precision=lax.Precision.HIGHEST, preferred_element_type=jnp.float32
    )
    image_part = jnp.dot(
        flat, image_flat.T, precision=lax.Precision.HIGHEST, preferred_element_type=jnp.float32
    )
    gram, image_gram = lax.psum((gram_part, image_part), ("gx", "gy"))
    cells = float(flat.shape[1] * lax.axis_size("gx") * lax.axis_size("gy"))
    gram = gram / cells
    image_gram = image_gram / cells
    lower = jnp.linalg.cholesky(gram)
    identity = jnp.eye(vectors_count, dtype=jnp.float32)
    inverse = lax.linalg.triangular_solve(lower, identity, left_side=True, lower=True)
    basis = jnp.dot(
        inverse, flat, precision=lax.Precision.HIGHEST, preferred_element_type=jnp.float32
    )
    projected = jnp.dot(
        jnp.dot(
            inverse, image_gram, precision=lax.Precision.HIGHEST, preferred_element_type=jnp.float32
        ),
        inverse.T,
        precision=lax.Precision.HIGHEST,
        preferred_element_type=jnp.float32,
    )
    return (basis.reshape(filtered.shape), projected)


def solution(mesh):
    in_specs = (P(None, None, "gy", "gx"), P(None, "gy", "gx"))
    out_specs = (P(None, None, "gy", "gx"), P())
    return jax.shard_map(
        per_device, mesh=mesh, in_specs=in_specs, out_specs=out_specs, check_vma=False
    )
```

profile of v0, /device:TPU:0, one launch (start us, length us, event | category | flops | bytes accessed | tf_op | source)
XLA Modules:
  0.0 187.1 jit_solution(10298983006626074201)
XLA Ops:
  9.4 3.0 %collective-permute-start = (f32[9,8,3,128]{3,1,2,0:T(8,128)S(1)}, f32[9,8,3,128]{3,1,2,0:T(8,128)S(1)}, u32[]{:S(2)}, u32[]{:S(2)}) collective-permute-start(f32[9,8,3,128]{3,1,2,0:T(8,128)S(1)} %get-tuple-element.23), channel_id=1, source_target_pairs={{0,2},{2,4},{4,6},{6,8},{8,10},{10,12},{12,14},{14,0},{1,3},{3,5},... | collective-permute-start | bytes 331784 | tf_op jit(solution)/shard_map/ppermute | solution.py:24
  12.5 3.1 %collective-permute-start.1 = (f32[9,8,3,128]{3,1,2,0:T(8,128)S(1)}, f32[9,8,3,128]{3,1,2,0:T(8,128)S(1)}, u32[]{:S(2)}, u32[]{:S(2)}) collective-permute-start(f32[9,8,3,128]{3,1,2,0:T(8,128)S(1)} %get-tuple-element.24), channel_id=1, source_target_pairs={{2,0},{4,2},{6,4},{8,6},{10,8},{12,10},{14,12},{0,14},{3,1},{5,3},... | collective-permute-start | bytes 331784 | tf_op jit(solution)/shard_map/ppermute | solution.py:27
  15.7 2.9 %collective-permute-done = f32[9,8,3,128]{3,1,2,0:T(8,128)S(1)} collective-permute-done((f32[9,8,3,128]{3,1,2,0:T(8,128)S(1)}, f32[9,8,3,128]{3,1,2,0:T(8,128)S(1)}, u32[]{:S(2)}, u32[]{:S(2)}) %collective-permute-start) | collective-permute-done | bytes 110624 | tf_op jit(solution)/shard_map/ppermute | solution.py:24
  23.0 3.8 %fusion = (f32[4,8,8,30,1]{4,2,3,1,0:T(8,128)}, f32[4,8,8,30,1]{4,2,3,1,0:T(8,128)}) fusion(f32[2,8,8,30,128]{4,2,3,1,0:T(8,128)S(1)} %get-tuple-element.21, f32[2,8,8,30,128]{4,2,3,1,0:T(8,128)S(1)} %get-tuple-element.22), kind=kLoop, calls=%fused_computation.24 | loop fusion | flops 15360 | bytes 3993600 | tf_op jit(solution)/shard_map/concatenate | solution.py:104
  26.9 3.9 %copy.76 = f32[4,8,8,30,1]{3,2,4,1,0:T(8,128)} copy(f32[4,8,8,30,1]{4,2,3,1,0:T(8,128)} %get-tuple-element.17) | data formatting | bytes 61440
  32.2 3.9 %copy.77 = f32[4,8,8,30,1]{3,2,4,1,0:T(8,128)} copy(f32[4,8,8,30,1]{4,2,3,1,0:T(8,128)} %get-tuple-element.18) | data formatting | bytes 61440
  36.6 3.8 %fusion.4 = f32[4,8,7,28,128]{4,2,3,1,0:T(8,128)} fusion(f32[2,8,8,30,128]{4,2,3,1,0:T(8,128)S(1)} %get-tuple-element.21, f32[2,8,8,30,128]{4,2,3,1,0:T(8,128)} %copy-done.1), kind=kLoop, calls=%fused_computation.28 | loop fusion | flops 802816 | bytes 7143424 | tf_op jit(solution)/shard_map/concatenate | solution.py:104
  42.4 4.0 %copy.52 = f32[4,8,8,30,1]{4,2,3,1,0:T(8,128)} copy(f32[4,8,8,30,1]{3,2,4,1,0:T(8,128)} %collective-permute-done.2) | data formatting | bytes 61440 | tf_op jit(solution)/shard_map/ppermute | solution.py:24
  46.5 4.0 %copy.54 = f32[4,8,8,30,1]{4,2,3,1,0:T(8,128)} copy(f32[4,8,8,30,1]{3,2,4,1,0:T(8,128)} %collective-permute-done.3) | data formatting | bytes 61440 | tf_op jit(solution)/shard_map/ppermute | solution.py:27
  50.5 11.6 %fusion.7 = f32[4,8,8,28,128]{4,2,3,1,0:T(8,128)} fusion(f32[2,8,8,30,128]{4,2,3,1,0:T(8,128)S(1)} %get-tuple-element.21, f32[2,8,8,30,128]{4,2,3,1,0:T(8,128)} %copy-done.1, f32[4,8,8,30,1]{4,2,3,1,0:T(8,128)} %copy.54, f32[4,8,8,30,1]{4,2,3,1,0:T(8,128)} %copy.52, f32[4,8,7,28,128]{4,2,3,1,0:T(8,128)} %fusion.4, f32[8,28,128]{2,0,1:T(8,128)S(1)} %copy-done.11), kind=kLoop, calls=%fused_computation.31 | loop fusion | flops 17432576 | bytes 10989568 | tf_op jit(solution)/shard_map/sub | solution.py:51
  62.1 3.0 %add_add_fusion = (f32[2,8,8,28,128]{4,2,3,1,0:T(8,128)S(1)}, f32[2,8,8,28,128]{4,2,3,1,0:T(8,128)S(1)}, f32[2,8,8,28,128]{4,2,3,1,0:T(8,128)S(1)}) fusion(f32[2,8,8,30,128]{4,2,3,1,0:T(8,128)S(1)} %copy-done.2, f32[2,8,28,128]{3,1,2,0:T(8,128)S(1)} %slice_bitcast_fusion, f32[2,8,28,128]{3,1,2,0:T(8,128)S(1)} %slice_bitcast_fusion.1, ...), kind=kLoop, calls=%fused_computation.68 | loop fusion | flops 6422528 | bytes 14221328 | tf_op jit(solution)/shard_map/add | solution.py:87
  66.4 3.7 %fusion.2 = (f32[4,8,8,28,1]{4,2,3,1,0:T(8,128)}, f32[4,8,8,28,1]{4,2,3,1,0:T(8,128)}) fusion(f32[2,8,8,28,128]{4,2,3,1,0:T(8,128)S(1)} %subtract_add_fusion, f32[2,8,8,28,128]{4,2,3,1,0:T(8,128)S(1)} %get-tuple-element.12), kind=kLoop, calls=%fused_computation.26 | loop fusion | flops 14336 | bytes 3727360 | tf_op jit(solution)/shard_map/concatenate | solution.py:104
  70.1 3.3 %copy.78 = f32[4,8,8,28,1]{3,2,4,1,0:T(8,128)S(1)} copy(f32[4,8,8,28,1]{4,2,3,1,0:T(8,128)} %get-tuple-element.19) | data formatting | bytes 57344
  74.9 3.2 %copy.79 = f32[4,8,8,28,1]{3,2,4,1,0:T(8,128)S(1)} copy(f32[4,8,8,28,1]{4,2,3,1,0:T(8,128)} %get-tuple-element.20) | data formatting | bytes 57344
  78.7 3.6 %fusion.16 = f32[4,8,7,26,128]{4,2,3,1,0:T(8,128)} fusion(f32[2,8,8,28,128]{4,2,3,1,0:T(8,128)} %copy-done.5, f32[2,8,8,28,128]{4,2,3,1,0:T(8,128)S(1)} %copy-done.4), kind=kLoop, calls=%fused_computation.46 | loop fusion | flops 745472 | bytes 6651904 | tf_op jit(solution)/shard_map/concatenate | solution.py:104
  82.3 3.1 %copy.56 = f32[4,8,8,28,1]{4,2,3,1,0:T(8,128)} copy(f32[4,8,8,28,1]{3,2,4,1,0:T(8,128)S(1)} %collective-permute-done.4) | data formatting | bytes 57344 | tf_op jit(solution)/shard_map/ppermute | solution.py:24
  85.4 3.0 %copy.58 = f32[4,8,8,28,1]{4,2,3,1,0:T(8,128)} copy(f32[4,8,8,28,1]{3,2,4,1,0:T(8,128)S(1)} %collective-permute-done.5) | data formatting | bytes 57344 | tf_op jit(solution)/shard_map/ppermute | solution.py:27
  88.5 9.6 %fusion.19 = f32[4,8,8,26,128]{4,2,3,1,0:T(8,128)S(1)} fusion(f32[2,8,8,28,128]{4,2,3,1,0:T(8,128)} %copy-done.5, f32[2,8,8,28,128]{4,2,3,1,0:T(8,128)S(1)} %copy-done.4, f32[4,8,8,28,1]{4,2,3,1,0:T(8,128)} %copy.58, f32[4,8,8,28,1]{4,2,3,1,0:T(8,128)} %copy.56, f32[4,8,7,26,128]{4,2,3,1,0:T(8,128)} %fusion.16, f32[8,26,128]{2,0,1:T(8,128)S(1)} %copy-done.12), kind=kLoop, calls=%fused_computation.49 | loop fusion | flops 16187392 | bytes 10223616 | tf_op jit(solution)/shard_map/sub | solution.py:51
  100.8 19.4 %all-reduce.9.cloned.1.call-done = f32[8,8,26,128]{3,0,2,1:T(8,128)} async-done(((f32[8,8,26,128]{3,0,2,1:T(8,128)}), f32[8,8,26,128]{3,0,2,1:T(8,128)}) %all-reduce.9.cloned.1.call-update) | async-done | bytes 851984 | tf_op jit(solution)/shard_map/psum | solution.py:118
  120.2 1.8 fusion.76
  122.5 1.8 collective-permute-start.6
  126.1 1.8 convolution_bitcast_fusion.1
  129.2 3.1 %convolution_bitcast_fusion = f32[8,8]{0,1:T(8,128)S(1)} fusion(f32[8,8,26,128]{3,0,2,1:T(8,128)S(1)} %copy-done, f32[8,8,26,1]{3,0,2,1:T(8,128)S(1)} %copy.67, f32[8,8,26,1]{3,0,2,1:T(8,128)S(1)} %copy.65, f32[8,7,24,128]{3,0,2,1:T(8,128)} %get-tuple-element.26, f32[8,7,24,128]{3,0,2,1:T(8,128)S(1)} %get-tuple-element.25, ...), kind=kOutput, calls=%fused_computation.75 | convolution fusion | flops 20840448 | bytes 7241984 | tf_op jit(solution)/shard_map/dot_general | solution.py:128
  132.4 42.2 %all-reduce.6 = (f32[8,8]{0,1:T(8,128)S(1)}, f32[8,8]{0,1:T(8,128)S(1)}) all-reduce(f32[8,8]{0,1:T(8,128)S(1)} %convolution_bitcast_fusion.1, f32[8,8]{0,1:T(8,128)S(1)} %convolution_bitcast_fusion), channel_id=1, replica_groups=mesh['gx'=2,'gy'=8,'cp'=2] {'gx','gy'}, use_global_device_ids=true, to_apply=%region_2.0 | all-reduce | flops 128 | bytes 1024 | tf_op jit(solution)/shard_map/psum | solution.py:131
  (84 shorter events, 26.1 us)
Async XLA Ops:
  7.2 113.0 %all-reduce.9.cloned.1.call-start = ((), (), s32[]{:S(2)}) async-start(), calls=%async_computation | async-start | bytes 1703936 | tf_op jit(solution)/shard_map/psum | solution.py:118
  9.4 9.2 %collective-permute-start = (f32[9,8,3,128]{3,1,2,0:T(8,128)S(1)}, f32[9,8,3,128]{3,1,2,0:T(8,128)S(1)}, u32[]{:S(2)}, u32[]{:S(2)}) collective-permute-start(f32[9,8,3,128]{3,1,2,0:T(8,128)S(1)} %get-tuple-element.23), channel_id=1, source_target_pairs={{0,2},{2,4},{4,6},{6,8},{8,10},{10,12},{12,14},{14,0},{1,3},{3,5},... | collective-permute-start | bytes 331784 | tf_op jit(solution)/shard_map/ppermute | solution.py:24
  12.5 7.1 %collective-permute-start.1 = (f32[9,8,3,128]{3,1,2,0:T(8,128)S(1)}, f32[9,8,3,128]{3,1,2,0:T(8,128)S(1)}, u32[]{:S(2)}, u32[]{:S(2)}) collective-permute-start(f32[9,8,3,128]{3,1,2,0:T(8,128)S(1)} %get-tuple-element.24), channel_id=1, source_target_pairs={{2,0},{4,2},{6,4},{8,6},{10,8},{12,10},{14,12},{0,14},{3,1},{5,3},... | collective-permute-start | bytes 331784 | tf_op jit(solution)/shard_map/ppermute | solution.py:27
  23.0 3.9 %copy-start.1 = (f32[2,8,8,30,128]{4,2,3,1,0:T(8,128)}, f32[2,8,8,30,128]{4,2,3,1,0:T(8,128)S(1)}, u32[]{:S(2)}) copy-start(f32[2,8,8,30,128]{4,2,3,1,0:T(8,128)S(1)} %get-tuple-element.22) | copy-start | bytes 5898244
  30.8 11.7 %collective-permute-start.2 = (f32[4,8,8,30,1]{3,2,4,1,0:T(8,128)}, f32[4,8,8,30,1]{3,2,4,1,0:T(8,128)}, u32[]{:S(2)}, u32[]{:S(2)}) collective-permute-start(f32[4,8,8,30,1]{3,2,4,1,0:T(8,128)} %copy.76), channel_id=1, source_target_pairs={{0,16},{16,0},{1,17},{17,1},{2,18},{18,2},{3,19},{19,3},{4,20},{20... | collective-permute-start | bytes 92168 | tf_op jit(solution)/shard_map/ppermute | solution.py:24
  36.1 10.3 %collective-permute-start.3 = (f32[4,8,8,30,1]{3,2,4,1,0:T(8,128)}, f32[4,8,8,30,1]{3,2,4,1,0:T(8,128)}, u32[]{:S(2)}, u32[]{:S(2)}) collective-permute-start(f32[4,8,8,30,1]{3,2,4,1,0:T(8,128)} %copy.77), channel_id=1, source_target_pairs={{16,0},{0,16},{17,1},{1,17},{18,2},{2,18},{19,3},{3,19},{20,4},{4,... | collective-permute-start | bytes 92168 | tf_op jit(solution)/shard_map/ppermute | solution.py:27
  42.4 8.1 %copy-start.11 = (f32[8,28,128]{2,0,1:T(8,128)S(1)}, f32[8,28,128]{2,0,1:T(8,128)}, u32[]{:S(2)}) copy-start(f32[8,28,128]{2,0,1:T(8,128)} %slice_add_fusion.2) | copy-start | bytes 344068
  50.5 11.6 %copy-start.2 = (f32[2,8,8,30,128]{4,2,3,1,0:T(8,128)S(1)}, f32[2,8,8,30,128]{4,2,3,1,0:T(8,128)}, u32[]{:S(2)}) copy-start(f32[2,8,8,30,128]{4,2,3,1,0:T(8,128)} %copy-done.1) | copy-start | bytes 5898244
  50.5 11.6 %copy-start.7 = (f32[8,8,28,128]{3,1,2,0:T(8,128)S(1)}, f32[8,8,28,128]{3,1,2,0:T(8,128)}, u32[]{:S(2)}) copy-start(f32[8,8,28,128]{3,1,2,0:T(8,128)} %slice.216) | copy-start | bytes 2752516
  65.1 1.3 copy-start.3
  65.5 4.6 %copy-start.5 = (f32[2,8,8,28,128]{4,2,3,1,0:T(8,128)}, f32[2,8,8,28,128]{4,2,3,1,0:T(8,128)S(1)}, u32[]{:S(2)}) copy-start(f32[2,8,8,28,128]{4,2,3,1,0:T(8,128)S(1)} %subtract_add_fusion) | copy-start | bytes 5505028
  70.1 8.7 %copy-start.4 = (f32[2,8,8,28,128]{4,2,3,1,0:T(8,128)S(1)}, f32[2,8,8,28,128]{4,2,3,1,0:T(8,128)}, u32[]{:S(2)}) copy-start(f32[2,8,8,28,128]{4,2,3,1,0:T(8,128)} %copy-done.3) | copy-start | bytes 5505028
  73.4 8.9 %collective-permute-start.4 = (f32[4,8,8,28,1]{3,2,4,1,0:T(8,128)S(1)}, f32[4,8,8,28,1]{3,2,4,1,0:T(8,128)S(1)}, u32[]{:S(2)}, u32[]{:S(2)}) collective-permute-start(f32[4,8,8,28,1]{3,2,4,1,0:T(8,128)S(1)} %copy.78), channel_id=1, source_target_pairs={{0,16},{16,0},{1,17},{17,1},{2,18},{18,2},{3,19},{19,3},{4,20},{20... | collective-permute-start | bytes 86024 | tf_op jit(solution)/shard_map/ppermute | solution.py:24
  78.1 7.3 %collective-permute-start.5 = (f32[4,8,8,28,1]{3,2,4,1,0:T(8,128)S(1)}, f32[4,8,8,28,1]{3,2,4,1,0:T(8,128)S(1)}, u32[]{:S(2)}, u32[]{:S(2)}) collective-permute-start(f32[4,8,8,28,1]{3,2,4,1,0:T(8,128)S(1)} %copy.79), channel_id=1, source_target_pairs={{16,0},{0,16},{17,1},{1,17},{18,2},{2,18},{19,3},{3,19},{20,4},{4,... | collective-permute-start | bytes 86024 | tf_op jit(solution)/shard_map/ppermute | solution.py:27
  82.3 6.1 %copy-start.12 = (f32[8,26,128]{2,0,1:T(8,128)S(1)}, f32[8,26,128]{2,0,1:T(8,128)}, u32[]{:S(2)}) copy-start(f32[8,26,128]{2,0,1:T(8,128)} %slice_add_fusion.3) | copy-start | bytes 319492
  88.4 9.7 %copy-start.6 = (f32[2,8,8,28,128]{4,2,3,1,0:T(8,128)S(1)}, f32[2,8,8,28,128]{4,2,3,1,0:T(8,128)}, u32[]{:S(2)}) copy-start(f32[2,8,8,28,128]{4,2,3,1,0:T(8,128)} %copy-done.5) | copy-start | bytes 5505028
  88.4 9.7 %copy-start.8 = (f32[8,8,26,128]{3,1,2,0:T(8,128)S(1)}, f32[8,8,26,128]{3,1,2,0:T(8,128)}, u32[]{:S(2)}) copy-start(f32[8,8,26,128]{3,1,2,0:T(8,128)} %slice.236) | copy-start | bytes 2555908
  88.4 9.7 %copy-start.9 = (f32[2,8,26,128]{3,1,2,0:T(8,128)S(1)}, f32[2,8,26,128]{3,1,2,0:T(8,128)}, u32[]{:S(2)}) copy-start(f32[2,8,26,128]{3,1,2,0:T(8,128)} %slice_bitcast_fusion.2) | copy-start | bytes 638980
  88.5 9.7 %copy-start.10 = (f32[2,8,26,128]{3,1,2,0:T(8,128)S(1)}, f32[2,8,26,128]{3,1,2,0:T(8,128)}, u32[]{:S(2)}) copy-start(f32[2,8,26,128]{3,1,2,0:T(8,128)} %slice_bitcast_fusion.3) | copy-start | bytes 638980
  98.1 2.6 %copy-start.13 = (f32[8,24,128]{2,1,0:T(8,128)S(1)}, f32[8,24,128]{2,1,0:T(8,128)}, u32[]{:S(2)}) copy-start(f32[8,24,128]{2,1,0:T(8,128)} %param.3) | copy-start | bytes 294916
  120.2 4.9 %copy-start = (f32[8,8,26,128]{3,0,2,1:T(8,128)S(1)}, f32[8,8,26,128]{3,0,2,1:T(8,128)}, u32[]{:S(2)}) copy-start(f32[8,8,26,128]{3,0,2,1:T(8,128)} %all-reduce.9.cloned.1.call-done) | copy-start | bytes 2555908
  122.5 5.4 %collective-permute-start.6 = (f32[8,8,26,1]{2,1,3,0:T(8,128)S(1)}, f32[8,8,26,1]{2,1,3,0:T(8,128)S(1)}, u32[]{:S(2)}, u32[]{:S(2)}) collective-permute-start(f32[8,8,26,1]{2,1,3,0:T(8,128)S(1)} %copy.64), channel_id=1, source_target_pairs={{0,16},{16,0},{1,17},{17,1},{2,18},{18,2},{3,19},{19,3},{4,20},{20... | collective-permute-start | bytes 19976 | tf_op jit(solution)/shard_map/ppermute | solution.py:24
  124.8 4.0 %collective-permute-start.7 = (f32[8,8,26,1]{2,1,3,0:T(8,128)S(1)}, f32[8,8,26,1]{2,1,3,0:T(8,128)S(1)}, u32[]{:S(2)}, u32[]{:S(2)}) collective-permute-start(f32[8,8,26,1]{2,1,3,0:T(8,128)S(1)} %copy.66), channel_id=1, source_target_pairs={{16,0},{0,16},{17,1},{1,17},{18,2},{2,18},{19,3},{3,19},{20,4},{4,... | collective-permute-start | bytes 19976 | tf_op jit(solution)/shard_map/ppermute | solution.py:27
Sparse Core Ops, SparseCore 0:
  100.8 19.2 all-reduce.8
where the time goes:
time: 187 us
  other arithmetic  45.6 us (24%)
  blocking collectives  42.2 us (23%)
  local copies, waits for them, and re-layouts  42.1 us (23%)
  waiting for transfers between devices  23.7 us (13%)
  between operations  14.3 us (8%)
  starting transfers between devices  12.5 us (7%)
  matrix products  6.75 us (4%)
    psum x1, blocking collectives, per_device(): gram, image_gram = lax.psum((gram_part, image_part), ('gx', 'gy'))  42.2 us
    sub x2, other arithmetic, apply_hamiltonian(): return (diag_shift + potential) * centre - kinetic_half * near  21.2 us
    psum x1, waiting for transfers between devices, per_device(): summed = lax.psum(running, 'cp')  19.4 us
    unnamed x35, local copies, waits for them, and re-layouts  18.4 us
    concatenate x4, other arithmetic, per_device(): jnp.concatenate([real_part, imag_part], axis=0)  14.9 us
    ppermute x4, starting transfers between devices, with_halo(): lax.ppermute(lax.slice_in_dim(block, block.shape[dim] - width, None, axis...  7.9 us
    ppermute x3, local copies, waits for them, and re-layouts, with_halo(): lax.ppermute(lax.slice_in_dim(block, block.shape[dim] - width, None, axis...  7.61 us
    ppermute x3, local copies, waits for them, and re-layouts, with_halo(): lax.ppermute(lax.slice_in_dim(block, 0, width, axis=dim), axis, backward)  7.56 us
  transfers between devices with their start and end apart: 9, of which 4 were waited for; matrix products, arithmetic and copies ran while one was open for 15% of the time, Pallas kernels for 0%

commit v1 on v0

v1 whole, which is shorter than its diff:
```python
import functools
import math

import jax
import jax.numpy as jnp
from jax import lax
from jax.experimental import pallas as pl
from jax.experimental.pallas import tpu as pltpu
from jax.sharding import PartitionSpec as P

POINTS = 4
ITERS = 3

diag_shift = 3.0
kinetic_half = 0.5
contour_centre = -1.0
contour_radius = 2.0

LANES = 128
SUB = 8
REACH = ITERS
GROUP = 16


def contour(index):
    angle = math.pi * (index + 0.5) / POINTS
    return (
        contour_centre + contour_radius * math.cos(angle),
        contour_radius * math.sin(angle),
        contour_radius / POINTS * math.cos(angle),
        contour_radius / POINTS * math.sin(angle),
    )


def coefficients(pot, index):
    shift_real, shift_imag, weight_real, weight_imag = contour(index)
    offset = shift_real - (diag_shift + pot)
    scale = 1.0 / (offset * offset + shift_imag * shift_imag)
    real = offset * scale
    imag = -shift_imag * scale
    return (
        kinetic_half * real,
        kinetic_half * imag,
        weight_real * real - weight_imag * imag,
        weight_real * imag + weight_imag * real,
    )


def lane_ids(shape=(SUB, LANES)):
    return lax.broadcasted_iota(jnp.int32, shape, len(shape) - 1)


def sub_ids():
    return lax.broadcasted_iota(jnp.int32, (SUB, LANES), 0)


def near_sums(above, here, below):
    out = []
    for z, value in enumerate(here):
        near = above[z] + below[z]
        near = near + (pltpu.roll(value, 1, 1) + pltpu.roll(value, LANES - 1, 1))
        if z > 0:
            near = near + here[z - 1]
        if z + 1 < len(here):
            near = near + here[z + 1]
        out.append(near)
    return out


def spread(ref, row):
    return ref[pl.ds(row, SUB, stride=0), :]


def strip_of(tile_at, nz):
    lane = lane_ids()
    col = lane % GROUP
    group = lane // GROUP
    low = (col >= REACH) & (col < 8)
    high = (col >= 8) & (col < 16 - REACH)
    out = jnp.zeros((SUB, LANES), jnp.float32)
    for z in range(nz):
        value = tile_at(z)
        first = pltpu.roll(value, (GROUP * z + REACH) % LANES, 1)
        last = pltpu.roll(value, (GROUP * z + 8 + 5) % LANES, 1)
        out = jnp.where(low & (group == z), first, out)
        out = jnp.where(high & (group == z), last, out)
    return out


def outer_lanes():
    col = lane_ids() % GROUP
    return (col < REACH) | (col >= GROUP - REACH)


def send_strip(strip):
    col = lane_ids() % GROUP
    return jnp.where(col < 8, pltpu.roll(strip, LANES - 10, 1), pltpu.roll(strip, 10, 1))


def pack_kernel(x_hbm, pot_ref, out_ref, buf, sem):
    cp = lax.axis_index("cp")
    rows = x_hbm.shape[1]
    nz = pot_ref.shape[0]
    vectors = x_hbm.shape[0] // nz
    copy = pltpu.make_async_copy(x_hbm.at[:, pl.ds(cp * (rows - SUB), SUB), :], buf, sem)
    copy.start()
    pot = pot_ref.reshape(nz * rows, LANES)
    for k in range(REACH):
        row = k + cp * (rows - 1 - 2 * k)
        out_ref[REACH * nz + k] = pot[pl.ds(row, nz, stride=rows), :]
    copy.wait()
    flat = buf.reshape(vectors * nz * SUB, LANES)
    for k in range(REACH):
        row = k + cp * (SUB - 1 - 2 * k)
        for z in range(nz):
            out_ref[k * nz + z] = flat[pl.ds(z * SUB + row, vectors, stride=nz * SUB), :]


def interior_kernel(
    x_hbm, pot_ref, part_ref, edge_ref, strip_ref, pot_strip_ref, xs, tab, ub, vb, sem
):
    cp = lax.axis_index("cp")
    rows = x_hbm.shape[1]
    nz = pot_ref.shape[0]
    vectors = x_hbm.shape[0] // nz
    height = xs.shape[1]
    local = rows // 2 + REACH
    copy = pltpu.make_async_copy(
        x_hbm.at[:, pl.ds(cp * (rows - height), height), :], xs, sem
    )
    copy.start()
    pot = pot_ref.reshape(nz * rows, LANES)
    table = tab.reshape(POINTS * 4 * local * nz, LANES)

    def fill(r, carry):
        tile = pot[pl.ds(r + cp * (rows - 1 - 2 * r), nz, stride=rows), :]
        for j in range(POINTS):
            for q, value in enumerate(coefficients(tile, j)):
                tab[(j * 4 + q) * local + r] = value
        return carry

    lax.fori_loop(0, local, fill, 0)
    copy.wait()
    flat = xs.reshape(vectors * nz * height, LANES)

    def x_at(r, z):
        return flat[pl.ds(z * height + (r + cp * (height - 1 - 2 * r)), vectors, stride=nz * height), :]

    def strips(r, carry):
        strip_ref[r] = strip_of(lambda z: x_at(r, z), nz)
        row = r + cp * (rows - 1 - 2 * r)
        pot_strip_ref[r] = strip_of(lambda z: spread(pot, z * rows + row), nz)
        return carry

    lax.fori_loop(0, local, strips, 0)

    def clear(r, carry):
        for z in range(nz):
            part_ref[r, z] = jnp.zeros((SUB, LANES), jnp.float32)
        return carry

    lax.fori_loop(0, part_ref.shape[0], clear, 0)

    def point(j, carry):
        def coef(q, r, z):
            return spread(table, ((j * 4 + q) * local + r) * nz + z)

        def first(r, inner):
            for z in range(nz):
                x = x_at(r, z)
                ub[0, r, z] = coef(0, r, z) * x
                ub[1, r, z] = coef(1, r, z) * x
            return inner

        lax.fori_loop(0, local, first, 0)

        def rows_of(ref, q, r):
            return [ref[q, r, z] for z in range(nz)]

        def second(r, inner):
            near = [
                near_sums(rows_of(ub, q, r - 1), rows_of(ub, q, r), rows_of(ub, q, r + 1))
                for q in range(2)
            ]
            for z in range(nz):
                rest = x_at(r, z) - near[0][z]
                real, imag = coef(0, r, z), coef(1, r, z)
                vb[0, r, z] = real * rest + imag * near[1][z]
                vb[1, r, z] = imag * rest - real * near[1][z]
            return inner

        lax.fori_loop(1, local - 1, second, 0)
        for r in range(1, REACH):
            for q in range(2):
                for z in range(nz):
                    edge_ref[j, q, r - 1, z] = vb[q, r, z]

        def third(r, inner):
            near = [
                near_sums(rows_of(vb, q, r - 1), rows_of(vb, q, r), rows_of(vb, q, r + 1))
                for q in range(2)
            ]
            for z in range(nz):
                add = coef(2, r, z) * (x_at(r, z) - near[0][z]) + coef(3, r, z) * near[1][z]
                part_ref[r - 2, z] = part_ref[r - 2, z] + add
            return inner

        lax.fori_loop(2, local - 2, third, 0)
        return carry

    lax.fori_loop(0, POINTS, point, 0)


def strip_kernel(recv_ref, strip_ref, pot_strip_ref, all_ref, pot_ref, send_ref, tmp):
    nz = recv_ref.shape[0] // REACH - 1
    local = strip_ref.shape[0]
    total = local + REACH
    sub = sub_ids()
    flat = recv_ref.reshape(recv_ref.shape[0] * SUB, LANES)
    pots = [jnp.zeros((SUB, LANES), jnp.float32) for _ in range(pot_ref.shape[0])]
    for ri in range(total):
        if ri < REACH:
            k = REACH - 1 - ri
            strip = strip_of(lambda z: recv_ref[k * nz + z], nz)
            pot = strip_of(lambda z: spread(flat, (REACH * nz + k) * SUB + z), nz)
        else:
            strip = strip_ref[ri - REACH]
            pot = pot_strip_ref[ri - REACH]
        all_ref[ri] = strip
        send_ref[ri] = send_strip(strip)
        pots[ri // SUB] = jnp.where(sub == ri % SUB, pot, pots[ri // SUB])
    for t, value in enumerate(pots):
        pot_ref[t] = value
        send_ref[total + t] = send_strip(value)


def border_kernel(own_ref, recv_ref, edge_ref, out_ref, tab, ub, vb):
    nz = own_ref.shape[0] // REACH - 1
    span = REACH + 2
    table = tab.reshape(4 * (span + 1) * nz, LANES)

    def x_at(r, z):
        return own_ref[r * nz + z] if r >= 0 else recv_ref[(-1 - r) * nz + z]

    for j in range(POINTS):
        for r in range(-REACH, 2):
            tile = own_ref[REACH * nz + r] if r >= 0 else recv_ref[REACH * nz - 1 - r]
            for q, value in enumerate(coefficients(tile, j)):
                tab[q * (span + 1) + r + REACH] = value

        def coef(q, r, z):
            return spread(table, (q * (span + 1) + r + REACH) * nz + z)

        for r in range(-REACH, 2):
            for z in range(nz):
                x = x_at(r, z)
                ub[0, r + REACH, z] = coef(0, r, z) * x
                ub[1, r + REACH, z] = coef(1, r, z) * x

        def rows_of(ref, q, r):
            return [ref[q, r + REACH, z] for z in range(nz)]

        for r in range(1 - REACH, 1):
            near = [
                near_sums(rows_of(ub, q, r - 1), rows_of(ub, q, r), rows_of(ub, q, r + 1))
                for q in range(2)
            ]
            for z in range(nz):
                rest = x_at(r, z) - near[0][z]
                real, imag = coef(0, r, z), coef(1, r, z)
                vb[0, r + REACH, z] = real * rest + imag * near[1][z]
                vb[1, r + REACH, z] = imag * rest - real * near[1][z]

        def later(q, r):
            if r >= 1:
                return [edge_ref[j, q, r - 1, z] for z in range(nz)]
            return rows_of(vb, q, r)

        for r in range(-1, 2):
            near = [near_sums(later(q, r - 1), later(q, r), later(q, r + 1)) for q in range(2)]
            for z in range(nz):
                add = coef(2, r, z) * (x_at(r, z) - near[0][z]) + coef(3, r, z) * near[1][z]
                if j == 0:
                    out_ref[r + 1, z] = add
                else:
                    out_ref[r + 1, z] = out_ref[r + 1, z] + add


def close_kernel(
    all_ref, pot_strip_ref, recv_ref, border_ref, part_ref, pot_ref,
    own_ref, packet_ref, tab, xb, ub, vb, fb, pb, sb,
):
    cp = lax.axis_index("cp")
    nz, rows, _ = pot_ref.shape
    half = rows // 2
    total = all_ref.shape[0]
    tiles = pot_strip_ref.shape[0]
    outer = outer_lanes()
    lane = lane_ids()
    pot = pot_ref.reshape(nz * rows, LANES)

    for ri in range(total):
        xb[ri] = jnp.where(outer, recv_ref[ri], all_ref[ri])
    for t in range(tiles):
        value = jnp.where(outer, recv_ref[total + t], pot_strip_ref[t])
        for j in range(POINTS):
            for q, item in enumerate(coefficients(value, j)):
                tab[(j * 4 + q) * tiles + t] = item
    table = tab.reshape(POINTS * 4 * tiles * SUB, LANES)

    def strip_near(ref, q, ri):
        value = ref[q, ri]
        near = ref[q, ri - 1] + ref[q, ri + 1]
        near = near + (pltpu.roll(value, 1, 1) + pltpu.roll(value, LANES - 1, 1))
        below = jnp.where(lane >= GROUP, pltpu.roll(value, GROUP, 1), 0.0)
        above = jnp.where(lane < (nz - 1) * GROUP, pltpu.roll(value, LANES - GROUP, 1), 0.0)
        return near + (below + above)

    def coef(j, q, ri):
        return spread(table, (j * 4 + q) * tiles * SUB + ri)

    for ri in range(2, total - 2):
        fb[ri] = jnp.zeros((SUB, LANES), jnp.float32)

    def point(j, carry):
        for ri in range(total):
            ub[0, ri] = coef(j, 0, ri) * xb[ri]
            ub[1, ri] = coef(j, 1, ri) * xb[ri]
        for ri in range(1, total - 1):
            near = [strip_near(ub, q, ri) for q in range(2)]
            rest = xb[ri] - near[0]
            real, imag = coef(j, 0, ri), coef(j, 1, ri)
            vb[0, ri] = real * rest + imag * near[1]
            vb[1, ri] = imag * rest - real * near[1]
        for ri in range(2, total - 2):
            near = [strip_near(vb, q, ri) for q in range(2)]
            fb[ri] = fb[ri] + (coef(j, 2, ri) * (xb[ri] - near[0]) + coef(j, 3, ri) * near[1])
        return carry

    lax.fori_loop(0, POINTS, point, 0)

    low = lane < REACH
    high = lane >= LANES - REACH

    def patch(r, value_at):
        strip = fb[r + REACH]
        for z in range(nz):
            right = pltpu.roll(strip, (LANES - GROUP * z - 13) % LANES, 1)
            left = pltpu.roll(strip, (2 * LANES - 1 - GROUP * z - 2) % LANES, 1)
            value = jnp.where(high, right, jnp.where(low, left, value_at(z)))
            pb[r + 1, z] = value
            sb[r + 1, z] = pltpu.roll(jnp.where(lane == LANES - 1, left, value), 1, 1) + pltpu.roll(
                jnp.where(lane == 0, right, value), LANES - 1, 1
            )

    for r in range(-1, 2):
        patch(r, lambda z: border_ref[r + 1, z])

    def patches(r, carry):
        patch(r, lambda z: part_ref[r - 2, z])
        return carry

    lax.fori_loop(2, half + 1, patches, 0)

    count = SUB // 2 + 1

    def sums(r, carry):
        grams, images = list(carry[0]), list(carry[1])
        row = r + cp * (rows - 1 - 2 * r)
        here = [pb[r + 1, z] for z in range(nz)]
        for z in range(nz):
            near = (pb[r, z] + pb[r + 2, z]) + sb[r + 1, z]
            if z > 0:
                near = near + here[z - 1]
            if z + 1 < nz:
                near = near + here[z + 1]
            value = here[z]
            image = (diag_shift + spread(pot, z * rows + row)) * value - kinetic_half * near
            own_ref[r + cp * (half - 1 - 2 * r), z] = value
            for s in range(count):
                other = value if s == 0 else pltpu.roll(value, SUB - s, 0)
                grams[s] = grams[s] + other * value
                images[s] = images[s] + other * image
        return tuple(grams), tuple(images)

    zero = tuple(jnp.zeros((SUB, LANES), jnp.float32) for _ in range(count))
    grams, images = lax.fori_loop(0, half, sums, (zero, zero))
    tile = jnp.zeros((SUB, LANES), jnp.float32)
    for s in range(count):
        tile = jnp.where(lane == s, jnp.sum(grams[s], axis=1, keepdims=True), tile)
        tile = jnp.where(lane == SUB + s, jnp.sum(images[s], axis=1, keepdims=True), tile)
    spun = pltpu.roll(tile, 0, 1, stride=GROUP, stride_axis=0)
    line = jnp.sum(spun, axis=0, keepdims=True)
    packet_ref[...] = jnp.broadcast_to(line[None], packet_ref.shape)


def finish_kernel(
    packet_ref, own_hbm, other_hbm, basis_ref, projected_ref, buf, splat, sems, *, cells
):
    cp = lax.axis_index("cp")
    half = own_hbm.shape[0]
    nz = own_hbm.shape[1]
    vectors = own_hbm.shape[2]
    copies = [
        pltpu.make_async_copy(own_hbm, buf.at[pl.ds(cp * half, half)], sems.at[0]),
        pltpu.make_async_copy(other_hbm, buf.at[pl.ds((1 - cp) * half, half)], sems.at[1]),
    ]
    for copy in copies:
        copy.start()
    lane = lane_ids()
    sub = sub_ids()
    line = jnp.sum(packet_ref[...], axis=0) / cells
    tile = jnp.where(lane // GROUP == sub, jnp.broadcast_to(line, (SUB, LANES)), 0.0)
    for shift in (4 * GROUP, 2 * GROUP, GROUP):
        tile = tile + pltpu.roll(tile, shift, 1)
    for s in range(SUB // 2 + 1, SUB):
        moved = pltpu.roll(pltpu.roll(tile, SUB - s, 0), 2 * s - SUB, 1)
        tile = jnp.where((lane == s) | (lane == SUB + s), moved, tile)

    def square(value):
        value = jnp.where(lane < SUB, value, 0.0)
        value = value + pltpu.roll(value, LANES - SUB, 1)
        return jnp.where(lane < SUB, pltpu.roll(value, 0, 1, stride=1, stride_axis=0), 0.0)

    gram = square(tile)
    image = square(pltpu.roll(tile, LANES - SUB, 1))
    work = gram + jnp.where(lane == sub + SUB, 1.0, 0.0) + pltpu.roll(image, 2 * SUB, 1)

    def column(value, k):
        return jnp.sum(jnp.where(lane == k, value, 0.0), axis=1, keepdims=True)

    root = jnp.zeros((SUB, 1), jnp.float32)
    ids = sub[:, :1]
    for k in range(SUB):
        pivot_row = work[k : k + 1, :]
        pivot = pivot_row[:, k : k + 1]
        root = jnp.where(ids == k, 1.0 / jnp.sqrt(pivot), root)
        factor = jnp.where(ids > k, column(work, k) / pivot, 0.0)
        work = work - factor * pivot_row
    work = work * root
    inverse = jnp.where(lane < SUB, pltpu.roll(work, LANES - SUB, 1), 0.0)
    mixed = jnp.where(lane < SUB, pltpu.roll(work, LANES - 2 * SUB, 1), 0.0)
    result = jnp.zeros((SUB, LANES), jnp.float32)
    for c in range(SUB):
        part = jnp.sum(mixed * inverse[c : c + 1, :], axis=1, keepdims=True)
        result = jnp.where(lane == c, part, result)
    projected_ref[...] = result[:, :SUB]
    for b in range(SUB):
        splat[b] = jnp.broadcast_to(column(inverse, b), (SUB, LANES))
    splats = splat.reshape(SUB * SUB, LANES)
    weights = [[spread(splats, b * SUB + a) for b in range(a + 1)] for a in range(vectors)]
    for copy in copies:
        copy.wait()
    flat = buf.reshape(2 * half * nz * vectors, LANES)

    def plane(z, carry):
        for block in range(2 * half // SUB):
            loads = [
                flat[pl.ds((block * SUB * nz + z) * vectors + b, SUB, stride=nz * vectors), :]
                for b in range(vectors)
            ]
            for a in range(vectors):
                value = weights[a][0] * loads[0]
                for b in range(1, a + 1):
                    value = value + weights[a][b] * loads[b]
                basis_ref[a, z, block * SUB : (block + 1) * SUB, :] = value
        return carry

    lax.fori_loop(0, nz, plane, 0)


def call(kernel, operands, outs, scratch, spaces, flops=0, **options):
    return pl.pallas_call(
        functools.partial(kernel, **options),
        out_shape=[jax.ShapeDtypeStruct(shape, jnp.float32) for shape in outs],
        in_specs=[pl.BlockSpec(memory_space=space) for space in spaces],
        out_specs=[pl.BlockSpec(memory_space=pltpu.VMEM) for _ in outs],
        scratch_shapes=scratch,
        cost_estimate=pl.CostEstimate(
            flops=flops,
            bytes_accessed=sum(value.size * 4 for value in operands)
            + sum(4 * math.prod(shape) for shape in outs),
            transcendentals=0,
        ),
    )(*operands)


def per_device(start_vectors, potential):
    vectors, nz, rows, columns = start_vectors.shape
    half = rows // 2
    local = half + REACH
    total = local + REACH
    height = -(-local // SUB) * SUB
    assert vectors == SUB and nz == SUB and columns == LANES
    assert lax.axis_size("cp") == 2 and rows % SUB == 0
    vmem, far = pltpu.VMEM, pl.ANY
    tile = (SUB, LANES)
    f32 = jnp.float32
    flat = start_vectors.reshape(vectors * nz, rows, columns)

    count = lax.axis_size("gy")
    swaps = []
    for g in range(count):
        swaps.append((2 * g, 2 * ((g - 1) % count) + 1))
        swaps.append((2 * g + 1, 2 * ((g + 1) % count)))
    (own_rows,) = call(
        pack_kernel, (flat, potential), [(REACH * (nz + 1),) + tile],
        [pltpu.VMEM((vectors * nz, SUB, LANES), f32), pltpu.SemaphoreType.DMA],
        (far, vmem),
    )
    far_rows = lax.ppermute(own_rows, ("gy", "cp"), swaps)
    part, edge, strip, pot_strip = call(
        interior_kernel, (flat, potential),
        [(local - 4, nz) + tile, (POINTS, 2, REACH - 1, nz) + tile, (local,) + tile, (local,) + tile],
        [
            pltpu.VMEM((vectors * nz, height, LANES), f32),
            pltpu.VMEM((POINTS * 4 * local,) + tile, f32),
            pltpu.VMEM((2, local, nz) + tile, f32),
            pltpu.VMEM((2, local, nz) + tile, f32),
            pltpu.SemaphoreType.DMA,
        ],
        (far, vmem), flops=10**8,
    )
    tiles = -(-total // SUB)
    strips, pot_strips, send = call(
        strip_kernel, (far_rows, strip, pot_strip),
        [(total,) + tile, (tiles,) + tile, (total + tiles,) + tile],
        [pltpu.VMEM(tile, f32)], (vmem,) * 3,
    )
    size = lax.axis_size("gx")
    ahead = [(i, (i + 1) % size) for i in range(size)]
    back = [(i, (i - 1) % size) for i in range(size)]
    recv = lax.ppermute(send, "gx", ahead)
    if size > 2:
        other = lax.ppermute(send, "gx", back)
        recv = jnp.where((jnp.arange(LANES) % GROUP) < GROUP // 2, recv, other)
    (border,) = call(
        border_kernel, (own_rows, far_rows, edge), [(REACH, nz) + tile],
        [
            pltpu.VMEM((4 * (REACH + 3),) + tile, f32),
            pltpu.VMEM((2, REACH + 3, nz) + tile, f32),
            pltpu.VMEM((2, REACH + 3, nz) + tile, f32),
        ],
        (vmem,) * 3, flops=3 * 10**7,
    )
    axes = ("gx", "gy", "cp")
    devices = math.prod(lax.axis_size(axis) for axis in axes)
    own, packet = call(
        close_kernel, (strips, pot_strips, recv, border, part, potential),
        [(half, nz) + tile, (devices, 1, LANES)],
        [
            pltpu.VMEM((POINTS * 4 * tiles,) + tile, f32),
            pltpu.VMEM((total,) + tile, f32),
            pltpu.VMEM((2, total) + tile, f32),
            pltpu.VMEM((2, total) + tile, f32),
            pltpu.VMEM((total,) + tile, f32),
            pltpu.VMEM((half + 2, nz) + tile, f32),
            pltpu.VMEM((half + 2, nz) + tile, f32),
        ],
        (vmem,) * 6, flops=10**7,
    )
    other = lax.ppermute(own, "cp", [(0, 1), (1, 0)])
    packets = lax.all_to_all(packet, axes, 0, 0, tiled=True)
    cells = float(nz * rows * columns * lax.axis_size("gx") * lax.axis_size("gy"))
    basis, projected = call(
        finish_kernel, (packets, own, other),
        [(vectors, nz, rows, columns), (vectors, vectors)],
        [
            pltpu.VMEM((rows, nz) + tile, f32),
            pltpu.VMEM((SUB,) + tile, f32),
            pltpu.SemaphoreType.DMA((2,)),
        ],
        (vmem, far, far), cells=cells,
    )
    return (basis, projected)


def solution(mesh):
    in_specs = (P(None, None, "gy", "gx"), P(None, "gy", "gx"))
    out_specs = (P(None, None, "gy", "gx"), P())
    return jax.shard_map(
        per_device, mesh=mesh, in_specs=in_specs, out_specs=out_specs, check_vma=False
    )
```

time: 187 us -> 54.5 us (0.29)
  other arithmetic: 45.6 us -> 0 us
  local copies, waits for them, and re-layouts: 42.1 us -> 2.03 us
  Pallas kernels: 0 us -> 33.5 us
  blocking collectives: 42.2 us -> 10.4 us
  waiting for transfers between devices: 23.7 us -> 0.42 us
  between operations: 14.3 us -> 0.67 us
  matrix products: 6.75 us -> 0 us
  starting transfers between devices: 12.5 us -> 7.03 us
    psum x1 -> x0, blocking collectives: 42.2 us -> none  [per_device(): gram, image_gram = lax.psum((gram_part, image_part), ('gx', 'gy'))]
    pallas_call x0 -> x6, Pallas kernels: none -> 33.5 us  [call(): pl.pallas_call(functools.partial(kernel, **options), out_shape=[jax.Shape...]
    sub x2 -> x0, other arithmetic: 21.2 us -> none  [apply_hamiltonian(): return (diag_shift + potential) * centre - kinetic_half * near]
    psum x1 -> x0, waiting for transfers between devices: 19.4 us -> none  [per_device(): summed = lax.psum(running, 'cp')]
    unnamed x35 -> x6, local copies, waits for them, and re-layouts: 18.4 us -> 2.03 us
    ppermute x6 -> x0, local copies, waits for them, and re-layouts: 15.2 us -> none  [the longest x3 7.61 us: with_halo(): lax.ppermute(lax.slice_in_dim(block, block.shape[dim] - width, None, axis...]
    concatenate x5 -> x0, other arithmetic: 15 us -> none  [the longest x4 14.9 us: per_device(): jnp.concatenate([real_part, imag_part], axis=0)]
    all_to_all x0 -> x1, blocking collectives: none -> 10.4 us  [per_device(): packets = lax.all_to_all(packet, axes, 0, 0, tiled=True)]
  transfers between devices with their start and end apart: 9 -> 3, of which waited for: 4 -> 1; matrix products, arithmetic and copies ran while one was open for 15% -> 0% of each run, Pallas kernels for 0% -> 36%
where the time goes in v1:
time: 54.5 us; the launch traced here: 54.1 us
  Pallas kernels  33.5 us (61%)
  blocking collectives  10.4 us (19%)
  starting transfers between devices  7.03 us (13%)
  local copies, waits for them, and re-layouts  2.03 us (4%)
  between operations  0.67 us (1%)
    pallas_call x6, Pallas kernels, call(): pl.pallas_call(functools.partial(kernel, **options), out_shape=[jax.Shape...  33.5 us
    all_to_all x1, blocking collectives, per_device(): packets = lax.all_to_all(packet, axes, 0, 0, tiled=True)  10.4 us
    ppermute x1, starting transfers between devices, per_device(): far_rows = lax.ppermute(own_rows, ('gy', 'cp'), swaps)  5.54 us
    unnamed x6, local copies, waits for them, and re-layouts  2.03 us
    ppermute x1, starting transfers between devices, per_device(): recv = lax.ppermute(send, 'gx', ahead)  1.49 us
  transfers between devices with their start and end apart: 3, of which 1 were waited for; matrix products, arithmetic and copies ran while one was open for 0% of the time, Pallas kernels for 36%

profile of v1, /device:TPU:0, one launch (start us, length us, event | category | flops | bytes accessed | tf_op | source)
XLA Modules:
  0.0 54.1 jit_solution(4823583533783738818)
XLA Ops:
  0.6 2.6 %shard_map.41.own_ref = f32[27,8,128]{2,1,0:T(8,128)} custom-call(f32[64,24,128]{2,1,0:T(8,128)} %bitcast.1, f32[8,24,128]{2,1,0:T(8,128)} %pot_ref.5), custom_call_target="tpu_custom_call" | custom-call | bytes 995328 | tf_op jit(solution)/shard_map/pallas_call | solution.py:473
  3.2 5.5 %collective-permute-start = (f32[27,8,128]{2,1,0:T(8,128)}, f32[27,8,128]{2,1,0:T(8,128)S(1)}, u32[]{:S(2)}, u32[]{:S(2)}) collective-permute-start(f32[27,8,128]{2,1,0:T(8,128)} %shard_map.41.own_ref), channel_id=1, source_target_pairs={{0,15},{1,2},{2,1},{3,4},{4,3},{5,6},{6,5},{7,8},{8,7},{9,10},{10,... | collective-permute-start | bytes 331784 | tf_op jit(solution)/shard_map/ppermute | solution.py:511
  8.7 16.5 %shard_map.42 = (f32[11,8,8,128]{3,2,1,0:T(8,128)}, f32[4,2,2,8,8,128]{5,4,3,2,1,0:T(8,128)}, f32[15,8,128]{2,1,0:T(8,128)}, f32[15,8,128]{2,1,0:T(8,128)}) custom-call(f32[64,24,128]{2,1,0:T(8,128)} %bitcast.2, f32[8,24,128]{2,1,0:T(8,128)} %pot_ref.5), custom_call_target="tpu_custom_call" | custom-call | flops 100000000 | bytes 1892352 | tf_op jit(solution)/shard_map/pallas_call | solution.py:473
  25.3 0.0 collective-permute-done.recv_ref
  25.3 0.0 copy-start
  25.3 0.6 %copy-done = f32[27,8,128]{2,1,0:T(8,128)} copy-done((f32[27,8,128]{2,1,0:T(8,128)}, f32[27,8,128]{2,1,0:T(8,128)S(1)}, u32[]{:S(2)}) %copy-start) | copy-done | bytes 110616
  25.9 1.8 %shard_map.43 = (f32[18,8,128]{2,1,0:T(8,128)}, f32[3,8,128]{2,1,0:T(8,128)}, f32[21,8,128]{2,1,0:T(8,128)}) custom-call(f32[27,8,128]{2,1,0:T(8,128)} %copy-done, f32[15,8,128]{2,1,0:T(8,128)} %get-tuple-element.11.strip_ref, f32[15,8,128]{2,1,0:T(8,128)} %get-tuple-element.12.pot_strip_ref), custom_call_target="tpu_custom_call" | custom-call | bytes 405504 | tf_op jit(solution)/shard_map/pallas_call | solution.py:473
  27.8 1.5 %collective-permute-start.1 = (f32[21,8,128]{2,1,0:T(8,128)}, f32[21,8,128]{2,1,0:T(8,128)S(1)}, u32[]{:S(2)}, u32[]{:S(2)}) collective-permute-start(f32[21,8,128]{2,1,0:T(8,128)} %get-tuple-element.15), channel_id=1, source_target_pairs={{0,16},{16,0},{1,17},{17,1},{2,18},{18,2},{3,19},{19,3},{4,20},{20... | collective-permute-start | bytes 258056 | tf_op jit(solution)/shard_map/ppermute | solution.py:533
  29.3 2.8 %shard_map.44.border_ref = f32[3,8,8,128]{3,2,1,0:T(8,128)} custom-call(f32[27,8,128]{2,1,0:T(8,128)} %shard_map.41.own_ref, f32[27,8,128]{2,1,0:T(8,128)} %copy-done, f32[4,2,2,8,8,128]{5,4,3,2,1,0:T(8,128)} %get-tuple-element.16.edge_ref), custom_call_target="tpu_custom_call" | custom-call | flops 30000000 | bytes 843776 | tf_op jit(solution)/shard_map/pallas_call | solution.py:473
  32.1 0.4 collective-permute-done.1.recv_ref
  32.5 0.0 copy-start.2
  32.5 0.6 %copy-done.2 = f32[21,8,128]{2,1,0:T(8,128)} copy-done((f32[21,8,128]{2,1,0:T(8,128)}, f32[21,8,128]{2,1,0:T(8,128)S(1)}, u32[]{:S(2)}) %copy-start.2) | copy-done | bytes 86040
  33.1 5.7 %shard_map.45 = (f32[12,8,8,128]{3,2,1,0:T(8,128)}, f32[32,1,128]{2,1,0:T(1,128)}) custom-call(f32[18,8,128]{2,1,0:T(8,128)} %get-tuple-element.13.all_ref, f32[3,8,128]{2,1,0:T(8,128)} %get-tuple-element.14.pot_strip_ref, f32[21,8,128]{2,1,0:T(8,128)} %copy-done.2, f32[3,8,8,128]{3,2,1,0:T(8,128)} %shard_map.44.border_ref, ...), custom_call_target="tpu_custom_call" | custom-call | flops 10000000 | bytes 1138688 | tf_op jit(solution)/shard_map/pallas_call | solution.py:473
  38.8 0.0 collective-permute-start.2
  38.8 10.4 %all_to_all.5.packet_ref = f32[32,1,128]{2,1,0:T(1,128)} all-to-all(f32[32,1,128]{2,1,0:T(1,128)} %get-tuple-element.18), channel_id=1, replica_groups=mesh['gx'=2,'gy'=8,'cp'=2] {'gx','gy','cp'}, dimensions={0} | all-to-all | bytes 32768 | tf_op jit(solution)/shard_map/all_to_all | solution.py:563
  49.1 0.0 collective-permute-done.2.other_hbm
  49.2 0.0 copy-start.1
  49.2 0.8 %copy-done.1 = f32[12,8,8,128]{3,2,1,0:T(8,128)} copy-done((f32[12,8,8,128]{3,2,1,0:T(8,128)}, f32[12,8,8,128]{3,2,1,0:T(8,128)S(1)}, u32[]{:S(2)}) %copy-start.1) | copy-done | bytes 393240
  49.9 4.1 %shard_map.46 = (f32[8,8,24,128]{3,2,1,0:T(8,128)}, f32[8,8]{1,0:T(8,128)}) custom-call(f32[32,1,128]{2,1,0:T(1,128)} %all_to_all.5.packet_ref, f32[12,8,8,128]{3,2,1,0:T(8,128)} %get-tuple-element.19.own_hbm, f32[12,8,8,128]{3,2,1,0:T(8,128)} %copy-done.1), custom_call_target="tpu_custom_call" | custom-call | bytes 1589504 | tf_op jit(solution)/shard_map/pallas_call | solution.py:473
Async XLA Ops:
  3.2 22.1 %collective-permute-start = (f32[27,8,128]{2,1,0:T(8,128)}, f32[27,8,128]{2,1,0:T(8,128)S(1)}, u32[]{:S(2)}, u32[]{:S(2)}) collective-permute-start(f32[27,8,128]{2,1,0:T(8,128)} %shard_map.41.own_ref), channel_id=1, source_target_pairs={{0,15},{1,2},{2,1},{3,4},{4,3},{5,6},{6,5},{7,8},{8,7},{9,10},{10,... | collective-permute-start | bytes 331784 | tf_op jit(solution)/shard_map/ppermute | solution.py:511
  25.3 0.6 %copy-start = (f32[27,8,128]{2,1,0:T(8,128)}, f32[27,8,128]{2,1,0:T(8,128)S(1)}, u32[]{:S(2)}) copy-start(f32[27,8,128]{2,1,0:T(8,128)S(1)} %collective-permute-done.recv_ref) | copy-start | bytes 331780
  27.8 4.7 %collective-permute-start.1 = (f32[21,8,128]{2,1,0:T(8,128)}, f32[21,8,128]{2,1,0:T(8,128)S(1)}, u32[]{:S(2)}, u32[]{:S(2)}) collective-permute-start(f32[21,8,128]{2,1,0:T(8,128)} %get-tuple-element.15), channel_id=1, source_target_pairs={{0,16},{16,0},{1,17},{17,1},{2,18},{18,2},{3,19},{19,3},{4,20},{20... | collective-permute-start | bytes 258056 | tf_op jit(solution)/shard_map/ppermute | solution.py:533
  32.5 0.6 %copy-start.2 = (f32[21,8,128]{2,1,0:T(8,128)}, f32[21,8,128]{2,1,0:T(8,128)S(1)}, u32[]{:S(2)}) copy-start(f32[21,8,128]{2,1,0:T(8,128)S(1)} %collective-permute-done.1.recv_ref) | copy-start | bytes 258052
  38.8 10.4 %collective-permute-start.2 = (f32[12,8,8,128]{3,2,1,0:T(8,128)}, f32[12,8,8,128]{3,2,1,0:T(8,128)S(1)}, u32[]{:S(2)}, u32[]{:S(2)}) collective-permute-start(f32[12,8,8,128]{3,2,1,0:T(8,128)} %get-tuple-element.19.own_hbm), channel_id=1, source_target_pairs={{0,1},{1,0},{2,3},{3,2},{4,5},{5,4},{6,7},{7,6},{8,9},{9,8},{10,11... | collective-permute-start | bytes 1179656 | tf_op jit(solution)/shard_map/ppermute | solution.py:562
  49.2 0.8 %copy-start.1 = (f32[12,8,8,128]{3,2,1,0:T(8,128)}, f32[12,8,8,128]{3,2,1,0:T(8,128)S(1)}, u32[]{:S(2)}) copy-start(f32[12,8,8,128]{3,2,1,0:T(8,128)S(1)} %collective-permute-done.2.other_hbm) | copy-start | bytes 1179652

commit v2 on v0

v2 whole, which is shorter than its diff:
```python
import functools
import math

import jax
import jax.numpy as jnp
from jax import lax
from jax.experimental import pallas as pl
from jax.experimental.pallas import tpu as pltpu
from jax.sharding import PartitionSpec as P

POINTS = 4
ITERS = 3

diag_shift = 3.0
kinetic_half = 0.5
contour_centre = -1.0
contour_radius = 2.0

LANES = 128
SUB = 8
REACH = ITERS
GROUP = 16
GRANT = 16 * 2**20
TABLES = 12
EDGE = 2


def contour(index):
    angle = math.pi * (index + 0.5) / POINTS
    return (
        contour_centre + contour_radius * math.cos(angle),
        contour_radius * math.sin(angle),
        contour_radius / POINTS * math.cos(angle),
        contour_radius / POINTS * math.sin(angle),
    )


def coefficients(pot, index):
    shift_real, shift_imag, weight_real, weight_imag = contour(index)
    offset = shift_real - (diag_shift + pot)
    scale = 1.0 / (offset * offset + shift_imag * shift_imag)
    real = offset * scale
    imag = -shift_imag * scale
    return (
        kinetic_half * real,
        kinetic_half * imag,
        weight_real * real - weight_imag * imag,
        weight_real * imag + weight_imag * real,
    )


def lane_ids():
    return lax.broadcasted_iota(jnp.int32, (SUB, LANES), 1)


def sub_ids():
    return lax.broadcasted_iota(jnp.int32, (SUB, LANES), 0)


def turn(value, shift):
    return pltpu.roll(value, shift % LANES, 1)


def spread(ref, row):
    return ref[pl.ds(row, SUB, stride=0), :]


def all_sublanes(value):
    for shift in (4, 2, 1):
        value = value + pltpu.roll(value, shift, 0)
    return value


def column_ids():
    return lane_ids() & (GROUP - 1)


def settle(packed):
    col = column_ids()
    low = (col >= REACH) & (col < 8)
    high = (col >= 8) & (col < GROUP - REACH)
    return jnp.where(low, packed, jnp.where(high, turn(packed, 10), 0.0))


def strip_of(tiles):
    lane = lane_ids()
    packed = jnp.zeros((SUB, LANES), jnp.float32)
    for z, value in enumerate(tiles):
        inside = ((lane + 2 - GROUP * z) & (LANES - 1)) < 10
        packed = jnp.where(inside, turn(value, GROUP * z + REACH), packed)
    return settle(packed)


def strip_of_layers(tile):
    moved = pltpu.roll(tile, REACH, 1, stride=GROUP, stride_axis=0)
    inside = ((lane_ids() + 2 - GROUP * sub_ids()) & (LANES - 1)) < 10
    return settle(all_sublanes(jnp.where(inside, moved, 0.0)))


def outer_lanes():
    col = column_ids()
    return (col < REACH) | (col >= GROUP - REACH)


def send_strip(strip):
    return jnp.where(column_ids() < 8, turn(strip, -10), turn(strip, 10))


def copy_rows(x_hbm, window, sems, height, cp):
    rows = x_hbm.shape[2]
    return [
        pltpu.make_async_copy(
            x_hbm.at[v, :, pl.ds(cp * (rows - height), height), :], window.at[:, v], sems.at[v]
        )
        for v in range(x_hbm.shape[0])
    ]


def pack_kernel(x_hbm, pot_hbm, out_ref, window, pot_buf, sems):
    cp = lax.axis_index("cp")
    vectors, nz, rows, _ = x_hbm.shape
    offset = cp * (rows - SUB)
    copies = copy_rows(x_hbm, window, sems, SUB, cp)
    copies.append(
        pltpu.make_async_copy(pot_hbm.at[:, pl.ds(offset, SUB), :], pot_buf, sems.at[vectors])
    )
    for copy in copies:
        copy.start()
    for copy in copies:
        copy.wait()
    flat = window.reshape(nz * vectors * SUB, LANES)
    pot = pot_buf.reshape(nz * SUB, LANES)
    for k in range(REACH):
        row = k + cp * (SUB - 1 - 2 * k)
        for z in range(nz):
            out_ref[k * nz + z] = flat[pl.ds(z * vectors * SUB + row, vectors, stride=SUB), :]
        out_ref[REACH * nz + k] = pot[pl.ds(row, nz, stride=SUB), :]


def add(total, value):
    return value if total is None else total + value


def fill_tables(tab, tile, slot):
    total = None
    sides = (tile, turn(tile, 1), turn(tile, -1))
    for j in range(POINTS):
        for d, side in enumerate(sides):
            values = coefficients(side, j)
            for q, value in enumerate(values):
                tab[slot(j * TABLES + 4 * d + q)] = value
            if d == 0:
                total = add(total, values[2])
    tab[slot(POINTS * TABLES)] = total


def first_step(coef, x, ub, r, nz):
    for z in range(nz):
        for j in range(POINTS):
            for q in range(2):
                ub[j, q, r, z] = coef(j, q, z) * x[z]


def cross(rows, z):
    above, here, below = rows
    near = above[z] + below[z]
    if z > 0:
        near = near + here[z - 1]
    if z + 1 < len(here):
        near = near + here[z + 1]
    return near


def second_step(coef, x, left, right, rows_of, store, nz):
    for j in range(POINTS):
        rows = [rows_of(j, q) for q in range(2)]
        for z in range(nz):
            near = [
                cross(rows[q], z)
                + (coef(j, 4 + q, z) * left[z] + coef(j, 8 + q, z) * right[z])
                for q in range(2)
            ]
            rest = x[z] - near[0]
            real, imag = coef(j, 0, z), coef(j, 1, z)
            store(j, 0, z, real * rest + imag * near[1])
            store(j, 1, z, imag * rest - real * near[1])


def third_step(coef, x, rows_of, nz):
    straight, ahead, back = [None] * nz, [None] * nz, [None] * nz
    for j in range(POINTS):
        rows = [rows_of(j, q) for q in range(2)]
        for z in range(nz):
            real, imag = rows[0][1][z], rows[1][1][z]
            straight[z] = add(
                straight[z],
                coef(j, 3, z) * cross(rows[1], z) - coef(j, 2, z) * cross(rows[0], z),
            )
            ahead[z] = add(ahead[z], coef(j, 11, z) * imag - coef(j, 10, z) * real)
            back[z] = add(back[z], coef(j, 7, z) * imag - coef(j, 6, z) * real)
    return [
        (coef(POINTS, 0, z) * x[z] + straight[z]) + (turn(ahead[z], 1) + turn(back[z], -1))
        for z in range(nz)
    ]


def interior_kernel(
    x_ref, pot_ref, part_ref, edge_ref, strip_ref, pot_strip_ref, window, xs, tab, ub, vb, sems
):
    cp = lax.axis_index("cp")
    vectors, nz, rows, _ = x_ref.shape
    height = window.shape[2]
    local = rows // 2 + REACH
    span = xs.shape[1]
    copies = copy_rows(x_ref, window, sems, height, cp)
    for copy in copies:
        copy.start()
    pot = pot_ref.reshape(nz * rows, LANES)
    table = tab.reshape((POINTS * TABLES + 1) * span * nz, LANES)
    for copy in copies:
        copy.wait()
    flat = window.reshape(nz * vectors * height, LANES)

    def coefs(r):
        def coef(j, q, z):
            return spread(table, ((j * TABLES + q) * span + r) * nz + z)

        return coef

    for r in range(local):
        tile = pot[pl.ds(r + cp * (rows - 1 - 2 * r), nz, stride=rows), :]
        fill_tables(tab, tile, lambda index: index * span + r)
        pot_strip_ref[r] = strip_of_layers(tile)
        tiles = []
        for z in range(nz):
            start = z * vectors * height + r + cp * (height - 1 - 2 * r)
            value = flat[pl.ds(start, vectors, stride=height), :]
            xs[0, r, z] = value
            xs[1, r, z] = turn(value, 1)
            xs[2, r, z] = turn(value, -1)
            tiles.append(value)
        strip_ref[r] = strip_of(tiles)

    def x_at(r, d=0):
        return [xs[d, r, z] for z in range(nz)]

    def around(ref, r):
        return lambda j, q: [[ref[j, q, r + d, z] for z in range(nz)] for d in (-1, 0, 1)]

    for r in range(local):
        first_step(coefs(r), x_at(r), ub, r, nz)

    def second(r, carry):
        def store(j, q, z, value):
            vb[j, q, r, z] = value

        second_step(coefs(r), x_at(r), x_at(r, 1), x_at(r, 2), around(ub, r), store, nz)
        return carry

    lax.fori_loop(1, local - 1, second, 0)
    for j in range(POINTS):
        for q in range(2):
            for r in range(1, REACH):
                for z in range(nz):
                    edge_ref[j, q, r - 1, z] = vb[j, q, r, z]

    def third(r, carry):
        for z, value in enumerate(third_step(coefs(r), x_at(r), around(vb, r), nz)):
            part_ref[r - 2, z] = value
        return carry

    lax.fori_loop(2, local - 2, third, 0)


def strip_kernel(recv_ref, strip_ref, pot_strip_ref, all_ref, pot_ref, send_ref):
    nz = recv_ref.shape[0] // REACH - 1
    local = strip_ref.shape[0]
    total = local + REACH
    pairs = total // 2
    sub = sub_ids()
    outer = outer_lanes()
    pots = [jnp.zeros((SUB, LANES), jnp.float32) for _ in range(pot_ref.shape[0])]
    sends = []
    for ri in range(total):
        if ri < REACH:
            k = REACH - 1 - ri
            strip = strip_of([recv_ref[k * nz + z] for z in range(nz)])
            pot = strip_of_layers(recv_ref[REACH * nz + k])
        else:
            strip = strip_ref[ri - REACH]
            pot = pot_strip_ref[ri - REACH]
        all_ref[ri] = strip
        sends.append(send_strip(strip))
        pots[ri // SUB] = jnp.where(sub == ri % SUB, pot, pots[ri // SUB])
    for ri in range(pairs):
        send_ref[ri] = jnp.where(outer, sends[ri], turn(sends[ri + pairs], 8))
    for t, value in enumerate(pots):
        pot_ref[t] = value
        send_ref[pairs + t] = send_strip(value)


def gram_sums(other_of, value, image, grams, images):
    for s in range(len(grams)):
        other = other_of if s == 0 else pltpu.roll(other_of, SUB - s, 0)
        grams[s] = add(grams[s], other * value)
        images[s] = add(images[s], other * image)


def border_kernel(
    own_ref, recv_ref, edge_ref, part_ref, pot_ref, out_ref, sums_ref, tab, xs, ub, vb
):
    cp = lax.axis_index("cp")
    nz, rows, _ = pot_ref.shape
    half = rows // 2
    span = REACH + 2
    table = tab.reshape((POINTS * TABLES + 1) * span * nz, LANES)

    def coefs(r):
        def coef(j, q, z):
            return spread(table, ((j * TABLES + q) * span + r + REACH) * nz + z)

        return coef

    def x_at(r):
        return [own_ref[r * nz + z] if r >= 0 else recv_ref[(-1 - r) * nz + z] for z in range(nz)]

    def around(ref, r):
        def one(j, q, row):
            if row >= 1 and ref is vb:
                return [edge_ref[j, q, row - 1, z] for z in range(nz)]
            return [ref[j, q, row + REACH, z] for z in range(nz)]

        return lambda j, q: [one(j, q, r + d) for d in (-1, 0, 1)]

    for r in range(-REACH, 2):
        tile = own_ref[REACH * nz + r] if r >= 0 else recv_ref[REACH * nz - 1 - r]
        fill_tables(tab, tile, lambda index: index * span + r + REACH)
    for r in range(-REACH, 2):
        first_step(coefs(r), x_at(r), ub, r + REACH, nz)
    for r in range(1 - REACH, 1):
        def store(j, q, z, value):
            vb[j, q, r + REACH, z] = value

        x = x_at(r)
        left = [turn(value, 1) for value in x]
        right = [turn(value, -1) for value in x]
        second_step(coefs(r), x, left, right, around(ub, r), store, nz)
    for r in range(-1, 2):
        for z, value in enumerate(third_step(coefs(r), x_at(r), around(vb, r), nz)):
            out_ref[r + 1, z] = value

    lane = lane_ids()
    kept = (lane >= EDGE) & (lane < LANES - EDGE)
    pot = pot_ref.reshape(nz * rows, LANES)
    count = SUB // 2 + 1
    grams, images = [None] * count, [None] * count

    def row_of(r):
        return [out_ref[r + 1, z] if r < 2 else part_ref[r - 2, z] for z in range(nz)]

    for r in range(half):
        row = r + cp * (rows - 1 - 2 * r)
        above, below = row_of(r - 1), row_of(r + 1)
        here = [jnp.where(kept, value, 0.0) for value in row_of(r)]
        for z in range(nz):
            value = here[z]
            near = cross((above, here, below), z) + (turn(value, 1) + turn(value, -1))
            image = (diag_shift + spread(pot, z * rows + row)) * value - kinetic_half * near
            gram_sums(value, value, image, grams, images)
    for s, value in enumerate(grams + images):
        sums_ref[s] = value


def close_kernel(
    all_ref, pot_strip_ref, recv_ref, border_ref, part_ref, sums_ref,
    own_ref, packet_ref, tab, xb, ub, vb, fb,
):
    cp = lax.axis_index("cp")
    nz, half = own_ref.shape[:2]
    total = all_ref.shape[0]
    pairs = total // 2
    tiles = pot_strip_ref.shape[0]
    lane = lane_ids()
    col = column_ids()
    outer = outer_lanes()
    lower = lane >= GROUP
    upper = lane < (nz - 1) * GROUP
    shifts = (0, 1, -1, GROUP, -GROUP)
    span = tiles * SUB

    for t in range(tiles):
        value = jnp.where(outer, recv_ref[pairs + t], pot_strip_ref[t])
        pot_strip = value
        tab[POINTS * 20 * tiles + t] = pot_strip
        for d, shift in enumerate(shifts):
            side = value if d == 0 else turn(value, shift)
            for j in range(POINTS):
                for q, item in enumerate(coefficients(side, j)):
                    tab[(j * 20 + d * 4 + q) * tiles + t] = item
    table = tab.reshape((POINTS * 20 + 1) * span, LANES)

    def coef(j, d, q, ri):
        return spread(table, (j * 20 + d * 4 + q) * span + ri)

    for ri in range(total):
        came = recv_ref[ri] if ri < pairs else turn(recv_ref[ri - pairs], -8)
        value = jnp.where(outer, came, all_ref[ri])
        xb[0, ri] = value
        if 1 <= ri < total - 1:
            xb[1, ri] = turn(value, 1)
            xb[2, ri] = turn(value, -1)
            xb[3, ri] = jnp.where(lower, turn(value, GROUP), 0.0)
            xb[4, ri] = jnp.where(upper, turn(value, -GROUP), 0.0)
        for j in range(POINTS):
            for q in range(2):
                ub[j, q, ri] = coef(j, 0, q, ri) * value

    for ri in range(1, total - 1):
        sides = [xb[d, ri] for d in range(5)]
        for j in range(POINTS):
            near = []
            for q in range(2):
                value = ub[j, q, ri - 1] + ub[j, q, ri + 1]
                for d in range(1, 5):
                    value = value + coef(j, d, q, ri) * sides[d]
                near.append(value)
            rest = sides[0] - near[0]
            real, imag = coef(j, 0, 0, ri), coef(j, 0, 1, ri)
            vb[j, 0, ri] = real * rest + imag * near[1]
            vb[j, 1, ri] = imag * rest - real * near[1]

    for ri in range(2, total - 2):
        parts = [None] * 5
        weight = None
        for j in range(POINTS):
            weight = add(weight, coef(j, 0, 2, ri))
            for d in range(5):
                if d == 0:
                    real, imag = [vb[j, q, ri - 1] + vb[j, q, ri + 1] for q in range(2)]
                else:
                    real, imag = vb[j, 0, ri], vb[j, 1, ri]
                parts[d] = add(parts[d], coef(j, d, 3, ri) * imag - coef(j, d, 2, ri) * real)
        value = weight * xb[0, ri] + parts[0]
        value = value + (turn(parts[1], -1) + turn(parts[2], 1))
        value = value + jnp.where(upper, turn(parts[3], -GROUP), 0.0)
        fb[ri] = value + jnp.where(lower, turn(parts[4], GROUP), 0.0)

    count = SUB // 2 + 1
    grams = [sums_ref[s] for s in range(count)]
    images = [sums_ref[count + s] for s in range(count)]
    whole = ((col >= REACH) & (col < REACH + EDGE)) | (
        (col >= GROUP - REACH - EDGE) & (col < GROUP - REACH)
    )
    edge = (lane < EDGE) | (lane >= LANES - EDGE)
    joined = (col >= GROUP - REACH) & (col < GROUP - REACH + EDGE)
    for r in range(half):
        ri = r + REACH
        value = fb[ri]
        left, right = turn(value, 1), turn(value, -1)
        near = (fb[ri - 1] + fb[ri + 1]) + (left + right)
        near = near + jnp.where(lower, turn(value, GROUP), 0.0)
        near = near + jnp.where(upper, turn(value, -GROUP), 0.0)
        pot = spread(table, POINTS * 20 * span + ri)
        image = (diag_shift + pot) * value - kinetic_half * near
        rest = jnp.where(
            col == REACH + EDGE, left, jnp.where(col == GROUP - REACH - EDGE - 1, right, 0.0)
        )
        image = jnp.where(whole, image, -kinetic_half * rest)
        gram_sums(value, jnp.where(whole, value, 0.0), image, grams, images)
        compact = jnp.where(joined, turn(value, 10), value)
        place = r + cp * (half - 1 - 2 * r)
        for z in range(nz):
            base = border_ref[r + 1, z] if r < 2 else part_ref[r - 2, z]
            moved = turn(compact, -EDGE - GROUP * z - (GROUP - REACH - EDGE))
            own_ref[z, place] = jnp.where(edge, moved, base)

    tile = jnp.zeros((SUB, LANES), jnp.float32)
    for s in range(count):
        tile = jnp.where(lane == s, jnp.sum(grams[s], axis=1, keepdims=True), tile)
        tile = jnp.where(lane == SUB + s, jnp.sum(images[s], axis=1, keepdims=True), tile)
    spun = pltpu.roll(tile, 0, 1, stride=GROUP, stride_axis=0)
    line = jnp.sum(spun, axis=0, keepdims=True)
    packet_ref[...] = jnp.broadcast_to(line[None], packet_ref.shape)


def factor_inverse(entry, size):
    work = [[entry(i, k) for k in range(i + 1)] for i in range(size)]
    root = []
    for k in range(size):
        root.append(lax.rsqrt(work[k][k]))
        for i in range(k + 1, size):
            work[i][k] = work[i][k] * root[k]
        for i in range(k + 1, size):
            for m in range(k + 1, i + 1):
                work[i][m] = work[i][m] - work[i][k] * work[m][k]
    inverse = [[None] * (i + 1) for i in range(size)]
    for i in range(size):
        inverse[i][i] = root[i]
        for k in range(i):
            total = None
            for m in range(k, i):
                total = add(total, work[i][m] * inverse[m][k])
            inverse[i][k] = -(total * root[i])
    return inverse


def finish_kernel(packet_ref, own_ref, other_ref, basis_hbm, projected_ref, buf, out, sems, *, cells):
    cp = lax.axis_index("cp")
    nz, half = own_ref.shape[:2]
    vectors = basis_hbm.shape[0]
    own_copy = pltpu.make_async_copy(own_ref, buf.at[:, pl.ds(cp * half, half)], sems.at[0])
    other_copy = pltpu.make_async_copy(
        other_ref, buf.at[:, pl.ds((1 - cp) * half, half)], sems.at[1]
    )
    own_copy.start()
    other_copy.start()
    lane = lane_ids()
    sub = sub_ids()
    line = packet_ref[0:SUB, :]
    for start in range(SUB, packet_ref.shape[0], SUB):
        line = line + packet_ref[start : start + SUB, :]
    line = all_sublanes(line) * (1.0 / cells)

    def entry(i, k):
        s = (i - k) % SUB
        at = GROUP * k + s if s <= SUB // 2 else GROUP * i + SUB - s
        return jnp.broadcast_to(line[:, at : at + 1], (SUB, LANES))

    inverse = factor_inverse(entry, vectors)
    own_copy.wait()
    other_copy.wait()
    flat = buf.reshape(nz * 2 * half * vectors, LANES)
    copies = []
    for z in range(nz):
        for block in range(2 * half // SUB):
            loads = [
                flat[pl.ds((z * 2 * half + block * SUB) * vectors + b, SUB, stride=vectors), :]
                for b in range(vectors)
            ]
            for a in range(vectors):
                value = None
                for b in range(a + 1):
                    value = add(value, inverse[a][b] * loads[b])
                out[a, z, block * SUB : (block + 1) * SUB, :] = value
        copies.append(pltpu.make_async_copy(out.at[:, z], basis_hbm.at[:, z], sems.at[2 + z]))
        copies[-1].start()

    tile = jnp.where((lane >> 4) == sub, line, 0.0)
    for shift in (4 * GROUP, 2 * GROUP, GROUP):
        tile = tile + turn(tile, shift)
    tile = turn(tile, -SUB)
    for s in range(SUB // 2 + 1, SUB):
        moved = turn(pltpu.roll(tile, SUB - s, 0), 2 * s - SUB)
        tile = jnp.where(lane == s, moved, tile)
    tile = jnp.where(lane < SUB, tile, 0.0)
    tile = tile + turn(tile, -SUB)
    image = jnp.where(lane < SUB, pltpu.roll(tile, 0, 1, stride=1, stride_axis=0), 0.0)
    whole = jnp.zeros((SUB, LANES), jnp.float32)
    mixed = None
    for b in range(vectors):
        column = jnp.zeros((SUB, LANES), jnp.float32)
        for a in range(b, vectors):
            column = jnp.where(sub == a, inverse[a][b], column)
        whole = jnp.where(lane == b, column, whole)
        mixed = add(mixed, column * image[b : b + 1, :])
    result = jnp.zeros((SUB, LANES), jnp.float32)
    for c in range(vectors):
        part = jnp.sum(mixed * whole[c : c + 1, :], axis=1, keepdims=True)
        result = jnp.where(lane == c, part, result)
    projected_ref[...] = result[:, :vectors]
    for copy in copies:
        copy.wait()


def call(kernel, operands, outs, scratch, spaces, flops=0, out_spaces=None, **options):
    return pl.pallas_call(
        functools.partial(kernel, **options),
        out_shape=[jax.ShapeDtypeStruct(shape, jnp.float32) for shape in outs],
        in_specs=[pl.BlockSpec(memory_space=space) for space in spaces],
        out_specs=[
            pl.BlockSpec(memory_space=space) for space in out_spaces or [pltpu.VMEM] * len(outs)
        ],
        scratch_shapes=scratch,
        compiler_params=pltpu.CompilerParams(vmem_limit_bytes=GRANT),
        cost_estimate=pl.CostEstimate(
            flops=flops,
            bytes_accessed=sum(value.size * 4 for value in operands)
            + sum(4 * math.prod(shape) for shape in outs),
            transcendentals=0,
        ),
    )(*operands)


def per_device(start_vectors, potential):
    vectors, nz, rows, columns = start_vectors.shape
    half = rows // 2
    local = half + REACH
    total = local + REACH
    height = -(-local // SUB) * SUB
    assert vectors == SUB and nz == SUB and columns == LANES
    assert lax.axis_size("cp") == 2 and rows % SUB == 0 and total % 2 == 0
    vmem, far, hbm = pltpu.VMEM, pl.ANY, pltpu.HBM
    tile = (SUB, LANES)

    def room(*shape):
        return pltpu.VMEM(shape + tile, jnp.float32)

    count = lax.axis_size("gy")
    swaps = []
    for g in range(count):
        swaps.append((2 * g, 2 * ((g - 1) % count) + 1))
        swaps.append((2 * g + 1, 2 * ((g + 1) % count)))
    (own_rows,) = call(
        pack_kernel, (start_vectors, potential), [(REACH * (nz + 1),) + tile],
        [room(nz, vectors), room(nz), pltpu.SemaphoreType.DMA((vectors + 1,))],
        (hbm, hbm),
    )
    far_rows = lax.ppermute(own_rows, ("gy", "cp"), swaps)
    tables = POINTS * TABLES + 1
    part, edge, strip, pot_strip = call(
        interior_kernel, (start_vectors, potential),
        [(local - 4, nz) + tile, (POINTS, 2, REACH - 1, nz) + tile, (local,) + tile, (local,) + tile],
        [
            pltpu.VMEM((nz, vectors, height, LANES), jnp.float32),
            room(3, local + 2, nz),
            room(tables * (local + 2)),
            room(POINTS, 2, local + 2, nz),
            room(POINTS, 2, local, nz),
            pltpu.SemaphoreType.DMA((vectors,)),
        ],
        (far, vmem), flops=10**8,
    )
    tiles = -(-total // SUB)
    strips, pot_strips, send = call(
        strip_kernel, (far_rows, strip, pot_strip),
        [(total,) + tile, (tiles,) + tile, (total // 2 + tiles,) + tile],
        [], (vmem,) * 3,
    )
    size = lax.axis_size("gx")
    ahead = [(i, (i + 1) % size) for i in range(size)]
    back = [(i, (i - 1) % size) for i in range(size)]
    recv = lax.ppermute(send, "gx", ahead)
    if size > 2:
        other = lax.ppermute(send, "gx", back)
        recv = jnp.where((jnp.arange(LANES) % 8) < 4, recv, other)
    sums = 2 * (SUB // 2 + 1)
    border, partial = call(
        border_kernel, (own_rows, far_rows, edge, part, potential),
        [(REACH, nz) + tile, (sums,) + tile],
        [
            room(tables * (REACH + 2)),
            room(1),
            room(POINTS, 2, REACH + 2, nz),
            room(POINTS, 2, REACH + 2, nz),
        ],
        (vmem,) * 5, flops=3 * 10**7,
    )
    axes = ("gx", "gy", "cp")
    devices = math.prod(lax.axis_size(axis) for axis in axes)
    own, packet = call(
        close_kernel, (strips, pot_strips, recv, border, part, partial),
        [(nz, half) + tile, (devices, 1, LANES)],
        [
            room((POINTS * 20 + 1) * tiles),
            room(5, total),
            room(POINTS, 2, total),
            room(POINTS, 2, total),
            room(total),
        ],
        (vmem,) * 6, flops=10**7,
    )
    other = lax.ppermute(own, "cp", [(0, 1), (1, 0)])
    packets = lax.all_to_all(packet, axes, 0, 0, tiled=True).reshape(devices, LANES)
    cells = float(nz * rows * columns * lax.axis_size("gx") * lax.axis_size("gy"))
    basis, projected = call(
        finish_kernel, (packets, own, other),
        [(vectors, nz, rows, columns), (vectors, vectors)],
        [
            room(nz, rows),
            pltpu.VMEM((vectors, nz, rows, columns), jnp.float32),
            pltpu.SemaphoreType.DMA((2 + nz,)),
        ],
        (vmem, vmem, vmem), out_spaces=(hbm, vmem), cells=cells,
    )
    return (basis, projected)


def solution(mesh):
    in_specs = (P(None, None, "gy", "gx"), P(None, "gy", "gx"))
    out_specs = (P(None, None, "gy", "gx"), P())
    return jax.shard_map(
        per_device, mesh=mesh, in_specs=in_specs, out_specs=out_specs, check_vma=False
    )
```

time: 187 us -> 30.9 us (0.17)
  other arithmetic: 45.6 us -> 0 us
  local copies, waits for them, and re-layouts: 42.1 us -> 2.02 us
  blocking collectives: 42.2 us -> 9.67 us
  waiting for transfers between devices: 23.7 us -> 1.34 us
  between operations: 14.3 us -> 0.7 us
  Pallas kernels: 0 us -> 9.8 us
  matrix products: 6.75 us -> 0 us
  starting transfers between devices: 12.5 us -> 7.17 us
    psum x1 -> x0, blocking collectives: 42.2 us -> none  [per_device(): gram, image_gram = lax.psum((gram_part, image_part), ('gx', 'gy'))]
    sub x2 -> x0, other arithmetic: 21.2 us -> none  [apply_hamiltonian(): return (diag_shift + potential) * centre - kinetic_half * near]
    psum x1 -> x0, waiting for transfers between devices: 19.4 us -> none  [per_device(): summed = lax.psum(running, 'cp')]
    unnamed x35 -> x6, local copies, waits for them, and re-layouts: 18.4 us -> 2.02 us
    ppermute x6 -> x0, local copies, waits for them, and re-layouts: 15.2 us -> none  [the longest x3 7.61 us: with_halo(): lax.ppermute(lax.slice_in_dim(block, block.shape[dim] - width, None, axis...]
    concatenate x5 -> x0, other arithmetic: 15 us -> none  [the longest x4 14.9 us: per_device(): jnp.concatenate([real_part, imag_part], axis=0)]
    pallas_call x0 -> x6, Pallas kernels: none -> 9.8 us  [call(): pl.pallas_call(functools.partial(kernel, **options), out_shape=[jax.Shape...]
    all_to_all x0 -> x1, blocking collectives: none -> 9.67 us  [per_device(): lax.all_to_all(packet, axes, 0, 0, tiled=True).reshape(devices, LANES)]
  transfers between devices with their start and end apart: 9 -> 3, of which waited for: 4 -> 1; matrix products, arithmetic and copies ran while one was open for 15% -> 0% of each run, Pallas kernels for 0% -> 19%
where the time goes in v2:
time: 30.9 us; the launch traced here: 30.7 us
  Pallas kernels  9.8 us (32%)
  blocking collectives  9.67 us (31%)
  starting transfers between devices  7.17 us (23%)
  local copies, waits for them, and re-layouts  2.02 us (7%)
  waiting for transfers between devices  1.34 us (4%)
  between operations  0.7 us (2%)
    pallas_call x6, Pallas kernels, call(): pl.pallas_call(functools.partial(kernel, **options), out_shape=[jax.Shape...  9.8 us
    all_to_all x1, blocking collectives, per_device(): lax.all_to_all(packet, axes, 0, 0, tiled=True).reshape(devices, LANES)  9.67 us
    ppermute x1, starting transfers between devices, per_device(): far_rows = lax.ppermute(own_rows, ('gy', 'cp'), swaps)  5.54 us
    unnamed x6, local copies, waits for them, and re-layouts  2.02 us
    ppermute x1, starting transfers between devices, per_device(): recv = lax.ppermute(send, 'gx', ahead)  1.56 us
    ppermute x1, waiting for transfers between devices, per_device(): recv = lax.ppermute(send, 'gx', ahead)  1.34 us
  transfers between devices with their start and end apart: 3, of which 1 were waited for; matrix products, arithmetic and copies ran while one was open for 0% of the time, Pallas kernels for 19%

profile of v2, /device:TPU:0, one launch (start us, length us, event | category | flops | bytes accessed | tf_op | source)
XLA Modules:
  0.0 30.7 jit_solution(18400882965599287302)
XLA Ops:
  0.6 0.0 copy-start
  0.6 1.1 %copy-done = f32[8,8,24,128]{3,2,1,0:T(8,128)S(1)} copy-done((f32[8,8,24,128]{3,2,1,0:T(8,128)S(1)}, f32[8,8,24,128]{3,2,1,0:T(8,128)}, u32[]{:S(2)}) %copy-start) | copy-done | bytes 786456
  1.8 0.0 copy-start.1
  1.8 0.9 %copy-done.1 = f32[8,24,128]{2,1,0:T(8,128)S(1)} copy-done((f32[8,24,128]{2,1,0:T(8,128)S(1)}, f32[8,24,128]{2,1,0:T(8,128)}, u32[]{:S(2)}) %copy-start.1) | copy-done | bytes 98328
  2.7 0.2 shard_map.41.own_ref
  2.8 5.5 %collective-permute-start = (f32[27,8,128]{2,1,0:T(8,128)S(1)}, f32[27,8,128]{2,1,0:T(8,128)S(1)}, u32[]{:S(2)}, u32[]{:S(2)}) collective-permute-start(f32[27,8,128]{2,1,0:T(8,128)S(1)} %shard_map.41.own_ref), channel_id=1, source_target_pairs={{0,15},{1,2},{2,1},{3,4},{4,3},{5,6},{6,5},{7,8},{8,7},{9,10},{10,... | collective-permute-start | bytes 331784 | tf_op jit(solution)/shard_map/ppermute | solution.py:618
  8.4 4.7 %shard_map.42 = (f32[11,8,8,128]{3,2,1,0:T(8,128)S(1)}, f32[4,2,2,8,8,128]{5,4,3,2,1,0:T(8,128)S(1)}, f32[15,8,128]{2,1,0:T(8,128)S(1)}, f32[15,8,128]{2,1,0:T(8,128)S(1)}) custom-call(f32[8,8,24,128]{3,2,1,0:T(8,128)S(1)} %copy-done, f32[8,24,128]{2,1,0:T(8,128)S(1)} %copy-done.1), custom_call_target="tpu_custom_call" | custom-call | flops 100000000 | bytes 1892352 | tf_op jit(solution)/shard_map/pallas_call | solution.py:576
  13.0 0.0 collective-permute-done.recv_ref
  13.0 0.0 copy-start.2
  13.1 0.3 shard_map.43
  13.3 1.6 %collective-permute-start.1 = (f32[12,8,128]{2,1,0:T(8,128)S(1)}, f32[12,8,128]{2,1,0:T(8,128)S(1)}, u32[]{:S(2)}, u32[]{:S(2)}) collective-permute-start(f32[12,8,128]{2,1,0:T(8,128)S(1)} %get-tuple-element.17), channel_id=1, source_target_pairs={{0,16},{16,0},{1,17},{17,1},{2,18},{18,2},{3,19},{19,3},{4,20},{20... | collective-permute-start | bytes 147464 | tf_op jit(solution)/shard_map/ppermute | solution.py:642
  14.9 0.0 copy-done.2
  14.9 1.3 %shard_map.44 = (f32[3,8,8,128]{3,2,1,0:T(8,128)S(1)}, f32[10,8,128]{2,1,0:T(8,128)S(1)}) custom-call(f32[27,8,128]{2,1,0:T(8,128)S(1)} %shard_map.41.own_ref, f32[27,8,128]{2,1,0:T(8,128)S(1)} %collective-permute-done.recv_ref, f32[4,2,2,8,8,128]{5,4,3,2,1,0:T(8,128)S(1)} %get-tuple-element.18.edge_ref, f32[11,8,8,128]{3,2,1,0:T(8,128)S(1)} %get-tuple-element.19.part_ref, ...), custom_call_target="tpu_custom_call" | custom-call | flops 30000000 | bytes 1343488 | tf_op jit(solution)/shard_map/pallas_call | solution.py:576
  16.1 1.3 %collective-permute-done.1.recv_ref = f32[12,8,128]{2,1,0:T(8,128)S(1)} collective-permute-done((f32[12,8,128]{2,1,0:T(8,128)S(1)}, f32[12,8,128]{2,1,0:T(8,128)S(1)}, u32[]{:S(2)}, u32[]{:S(2)}) %collective-permute-start.1) | collective-permute-done | bytes 49184 | tf_op jit(solution)/shard_map/ppermute | solution.py:642
  17.5 1.0 %shard_map.45 = (f32[8,12,8,128]{3,2,1,0:T(8,128)S(1)}, f32[32,1,128]{2,1,0:T(1,128)S(1)}) custom-call(f32[18,8,128]{2,1,0:T(8,128)S(1)} %get-tuple-element.15.all_ref, f32[3,8,128]{2,1,0:T(8,128)S(1)} %get-tuple-element.16.pot_strip_ref, f32[12,8,128]{2,1,0:T(8,128)S(1)} %collective-permute-done.1.recv_ref, ...), custom_call_target="tpu_custom_call" | custom-call | flops 10000000 | bytes 1044480 | tf_op jit(solution)/shard_map/pallas_call | solution.py:576
  18.5 0.1 collective-permute-start.2
  18.6 9.7 %all_to_all.5 = f32[32,1,128]{2,1,0:T(1,128)S(1)} all-to-all(f32[32,1,128]{2,1,0:T(1,128)S(1)} %get-tuple-element.22), channel_id=1, replica_groups=mesh['gx'=2,'gy'=8,'cp'=2] {'gx','gy','cp'}, dimensions={0} | all-to-all | bytes 32768 | tf_op jit(solution)/shard_map/all_to_all | solution.py:673
  28.3 0.0 collective-permute-done.2.other_ref
  28.3 2.4 %shard_map.46 = (f32[8,8,24,128]{3,2,1,0:T(8,128)}, f32[8,8]{1,0:T(8,128)}) custom-call(f32[32,128]{1,0:T(8,128)S(1)} %bitcast.1, f32[8,12,8,128]{3,2,1,0:T(8,128)S(1)} %get-tuple-element.23.own_ref, f32[8,12,8,128]{3,2,1,0:T(8,128)S(1)} %collective-permute-done.2.other_ref), custom_call_target="tpu_custom_call" | custom-call | bytes 1589504 | tf_op jit(solution)/shard_map/pallas_call | solution.py:576
Async XLA Ops:
  0.6 1.1 %copy-start = (f32[8,8,24,128]{3,2,1,0:T(8,128)S(1)}, f32[8,8,24,128]{3,2,1,0:T(8,128)}, u32[]{:S(2)}) copy-start(f32[8,8,24,128]{3,2,1,0:T(8,128)} %x_ref.1) | copy-start | bytes 2359300
  1.8 0.9 %copy-start.1 = (f32[8,24,128]{2,1,0:T(8,128)S(1)}, f32[8,24,128]{2,1,0:T(8,128)}, u32[]{:S(2)}) copy-start(f32[8,24,128]{2,1,0:T(8,128)} %pot_ref.3) | copy-start | bytes 294916
  2.8 10.2 %collective-permute-start = (f32[27,8,128]{2,1,0:T(8,128)S(1)}, f32[27,8,128]{2,1,0:T(8,128)S(1)}, u32[]{:S(2)}, u32[]{:S(2)}) collective-permute-start(f32[27,8,128]{2,1,0:T(8,128)S(1)} %shard_map.41.own_ref), channel_id=1, source_target_pairs={{0,15},{1,2},{2,1},{3,4},{4,3},{5,6},{6,5},{7,8},{8,7},{9,10},{10,... | collective-permute-start | bytes 331784 | tf_op jit(solution)/shard_map/ppermute | solution.py:618
  13.0 1.8 %copy-start.2 = (f32[8,24,128]{2,1,0:T(8,128)S(1)}, f32[8,24,128]{2,1,0:T(8,128)}, u32[]{:S(2)}) copy-start(f32[8,24,128]{2,1,0:T(8,128)} %pot_ref.3) | copy-start | bytes 294916
  13.3 4.2 %collective-permute-start.1 = (f32[12,8,128]{2,1,0:T(8,128)S(1)}, f32[12,8,128]{2,1,0:T(8,128)S(1)}, u32[]{:S(2)}, u32[]{:S(2)}) collective-permute-start(f32[12,8,128]{2,1,0:T(8,128)S(1)} %get-tuple-element.17), channel_id=1, source_target_pairs={{0,16},{16,0},{1,17},{17,1},{2,18},{18,2},{3,19},{19,3},{4,20},{20... | collective-permute-start | bytes 147464 | tf_op jit(solution)/shard_map/ppermute | solution.py:642
  18.5 9.8 %collective-permute-start.2 = (f32[8,12,8,128]{3,2,1,0:T(8,128)S(1)}, f32[8,12,8,128]{3,2,1,0:T(8,128)S(1)}, u32[]{:S(2)}, u32[]{:S(2)}) collective-permute-start(f32[8,12,8,128]{3,2,1,0:T(8,128)S(1)} %get-tuple-element.23.own_ref), channel_id=1, source_target_pairs={{0,1},{1,0},{2,3},{3,2},{4,5},{5,4},{6,7},{7,6},{8,9},{9,8},{10,11... | collective-permute-start | bytes 1179656 | tf_op jit(solution)/shard_map/ppermute | solution.py:672

commit v3 on v2

--- a/solution.py
+++ b/solution.py
@@ -504,16 +504,16 @@
     return inverse
 
 
-def finish_kernel(packet_ref, own_ref, other_ref, basis_hbm, projected_ref, buf, out, sems, *, cells):
+def finish_kernel(
+    packet_ref, own_ref, other_ref, basis_hbm, projected_hbm, buf, out, small, sems, *, cells
+):
     cp = lax.axis_index("cp")
     nz, half = own_ref.shape[:2]
     vectors = basis_hbm.shape[0]
-    own_copy = pltpu.make_async_copy(own_ref, buf.at[:, pl.ds(cp * half, half)], sems.at[0])
-    other_copy = pltpu.make_async_copy(
-        other_ref, buf.at[:, pl.ds((1 - cp) * half, half)], sems.at[1]
-    )
-    own_copy.start()
-    other_copy.start()
+    for z in range(nz):
+        for r in range(half):
+            buf[z, cp * half + r] = own_ref[z, r]
+            buf[z, (1 - cp) * half + r] = other_ref[z, r]
     lane = lane_ids()
     sub = sub_ids()
     line = packet_ref[0:SUB, :]
@@ -527,8 +527,6 @@
         return jnp.broadcast_to(line[:, at : at + 1], (SUB, LANES))
 
     inverse = factor_inverse(entry, vectors)
-    own_copy.wait()
-    other_copy.wait()
     flat = buf.reshape(nz * 2 * half * vectors, LANES)
     copies = []
     for z in range(nz):
@@ -542,7 +540,7 @@
                 for b in range(a + 1):
                     value = add(value, inverse[a][b] * loads[b])
                 out[a, z, block * SUB : (block + 1) * SUB, :] = value
-        copies.append(pltpu.make_async_copy(out.at[:, z], basis_hbm.at[:, z], sems.at[2 + z]))
+        copies.append(pltpu.make_async_copy(out.at[:, z], basis_hbm.at[:, z], sems.at[z]))
         copies[-1].start()
 
     tile = jnp.where((lane >> 4) == sub, line, 0.0)
@@ -567,12 +565,16 @@
     for c in range(vectors):
         part = jnp.sum(mixed * whole[c : c + 1, :], axis=1, keepdims=True)
         result = jnp.where(lane == c, part, result)
-    projected_ref[...] = result[:, :vectors]
+    small[...] = result[:, :vectors]
+    copies.append(pltpu.make_async_copy(small, projected_hbm, sems.at[nz]))
+    copies[-1].start()
     for copy in copies:
         copy.wait()
 
 
-def call(kernel, operands, outs, scratch, spaces, flops=0, out_spaces=None, **options):
+def call(
+    kernel, operands, outs, scratch, spaces, flops=0, out_spaces=None, grant=GRANT, **options
+):
     return pl.pallas_call(
         functools.partial(kernel, **options),
         out_shape=[jax.ShapeDtypeStruct(shape, jnp.float32) for shape in outs],
@@ -581,7 +583,7 @@
             pl.BlockSpec(memory_space=space) for space in out_spaces or [pltpu.VMEM] * len(outs)
         ],
         scratch_shapes=scratch,
-        compiler_params=pltpu.CompilerParams(vmem_limit_bytes=GRANT),
+        compiler_params=pltpu.CompilerParams(vmem_limit_bytes=grant),
         cost_estimate=pl.CostEstimate(
             flops=flops,
             bytes_accessed=sum(value.size * 4 for value in operands)
@@ -611,7 +613,9 @@
         swaps.append((2 * g, 2 * ((g - 1) % count) + 1))
         swaps.append((2 * g + 1, 2 * ((g + 1) % count)))
     (own_rows,) = call(
-        pack_kernel, (start_vectors, potential), [(REACH * (nz + 1),) + tile],
+        pack_kernel,
+        [pltpu.with_memory_space_constraint(value, hbm) for value in (start_vectors, potential)],
+        [(REACH * (nz + 1),) + tile],
         [room(nz, vectors), room(nz), pltpu.SemaphoreType.DMA((vectors + 1,))],
         (hbm, hbm),
     )
@@ -678,9 +682,10 @@
         [
             room(nz, rows),
             pltpu.VMEM((vectors, nz, rows, columns), jnp.float32),
-            pltpu.SemaphoreType.DMA((2 + nz,)),
+            pltpu.VMEM((vectors, vectors), jnp.float32),
+            pltpu.SemaphoreType.DMA((nz + 1,)),
         ],
-        (vmem, vmem, vmem), out_spaces=(hbm, vmem), cells=cells,
+        (vmem, vmem, vmem), out_spaces=(hbm, hbm), cells=cells,
     )
     return (basis, projected)
 

time: 30.9 us -> 28.9 us (0.935)
  local copies, waits for them, and re-layouts: 2.02 us -> 0.01 us
    unnamed x6 -> x4, local copies, waits for them, and re-layouts: 2.02 us -> 0.01 us
  transfers between devices with their start and end apart: 3 -> 3, of which waited for: 1 -> 1; matrix products, arithmetic and copies ran while one was open for 0% -> 0% of each run, Pallas kernels for 19% -> 21%
where the time goes in v3:
time: 28.9 us; the launch traced here: 28.8 us
  Pallas kernels  9.87 us (34%)
  blocking collectives  9.67 us (33%)
  starting transfers between devices  7.17 us (25%)
  waiting for transfers between devices  1.35 us (5%)
  between operations  0.7 us (2%)
    pallas_call x6, Pallas kernels, call(): pl.pallas_call(functools.partial(kernel, **options), out_shape=[jax.Shape...  9.87 us
    all_to_all x1, blocking collectives, per_device(): lax.all_to_all(packet, axes, 0, 0, tiled=True).reshape(devices, LANES)  9.67 us
    ppermute x1, starting transfers between devices, per_device(): far_rows = lax.ppermute(own_rows, ('gy', 'cp'), swaps)  5.54 us
    ppermute x1, starting transfers between devices, per_device(): recv = lax.ppermute(send, 'gx', ahead)  1.56 us
    ppermute x1, waiting for transfers between devices, per_device(): recv = lax.ppermute(send, 'gx', ahead)  1.34 us
  transfers between devices with their start and end apart: 3, of which 1 were waited for; matrix products, arithmetic and copies ran while one was open for 0% of the time, Pallas kernels for 21%

profile of v3, /device:TPU:0, one launch (start us, length us, event | category | flops | bytes accessed | tf_op | source)
XLA Modules:
  0.0 28.8 jit_solution(6347713057316748853)
XLA Ops:
  0.6 0.0 copy-start.1
  0.6 0.0 copy-start
  0.6 1.1 %shard_map.41.own_ref = f32[27,8,128]{2,1,0:T(8,128)S(1)} custom-call(f32[8,8,24,128]{3,2,1,0:T(8,128)} %x_ref.1, f32[8,24,128]{2,1,0:T(8,128)} %pot_ref.3), custom_call_target="tpu_custom_call" | custom-call | bytes 995328 | tf_op jit(solution)/shard_map/pallas_call | solution.py:578
  1.7 5.5 %collective-permute-start = (f32[27,8,128]{2,1,0:T(8,128)S(1)}, f32[27,8,128]{2,1,0:T(8,128)S(1)}, u32[]{:S(2)}, u32[]{:S(2)}) collective-permute-start(f32[27,8,128]{2,1,0:T(8,128)S(1)} %shard_map.41.own_ref), channel_id=1, source_target_pairs={{0,15},{1,2},{2,1},{3,4},{4,3},{5,6},{6,5},{7,8},{8,7},{9,10},{10,... | collective-permute-start | bytes 331784 | tf_op jit(solution)/shard_map/ppermute | solution.py:622
  7.3 0.0 copy-done.1
  7.3 0.0 copy-done
  7.3 4.7 %shard_map.42 = (f32[11,8,8,128]{3,2,1,0:T(8,128)S(1)}, f32[4,2,2,8,8,128]{5,4,3,2,1,0:T(8,128)S(1)}, f32[15,8,128]{2,1,0:T(8,128)S(1)}, f32[15,8,128]{2,1,0:T(8,128)S(1)}) custom-call(f32[8,8,24,128]{3,2,1,0:T(8,128)S(1)} %copy-done, f32[8,24,128]{2,1,0:T(8,128)S(1)} %copy-done.1), custom_call_target="tpu_custom_call" | custom-call | flops 100000000 | bytes 1892352 | tf_op jit(solution)/shard_map/pallas_call | solution.py:578
  12.0 0.0 collective-permute-done.recv_ref
  12.0 0.2 shard_map.43
  12.2 1.6 %collective-permute-start.1 = (f32[12,8,128]{2,1,0:T(8,128)S(1)}, f32[12,8,128]{2,1,0:T(8,128)S(1)}, u32[]{:S(2)}, u32[]{:S(2)}) collective-permute-start(f32[12,8,128]{2,1,0:T(8,128)S(1)} %get-tuple-element.17), channel_id=1, source_target_pairs={{0,16},{16,0},{1,17},{17,1},{2,18},{18,2},{3,19},{19,3},{4,20},{20... | collective-permute-start | bytes 147464 | tf_op jit(solution)/shard_map/ppermute | solution.py:646
  13.8 1.2 %shard_map.44 = (f32[3,8,8,128]{3,2,1,0:T(8,128)S(1)}, f32[10,8,128]{2,1,0:T(8,128)S(1)}) custom-call(f32[27,8,128]{2,1,0:T(8,128)S(1)} %shard_map.41.own_ref, f32[27,8,128]{2,1,0:T(8,128)S(1)} %collective-permute-done.recv_ref, f32[4,2,2,8,8,128]{5,4,3,2,1,0:T(8,128)S(1)} %get-tuple-element.18.edge_ref, f32[11,8,8,128]{3,2,1,0:T(8,128)S(1)} %get-tuple-element.19.part_ref, ...), custom_call_target="tpu_custom_call" | custom-call | flops 30000000 | bytes 1343488 | tf_op jit(solution)/shard_map/pallas_call | solution.py:578
  15.0 1.3 %collective-permute-done.1.recv_ref = f32[12,8,128]{2,1,0:T(8,128)S(1)} collective-permute-done((f32[12,8,128]{2,1,0:T(8,128)S(1)}, f32[12,8,128]{2,1,0:T(8,128)S(1)}, u32[]{:S(2)}, u32[]{:S(2)}) %collective-permute-start.1) | collective-permute-done | bytes 49184 | tf_op jit(solution)/shard_map/ppermute | solution.py:646
  16.4 1.0 %shard_map.45 = (f32[8,12,8,128]{3,2,1,0:T(8,128)S(1)}, f32[32,1,128]{2,1,0:T(1,128)S(1)}) custom-call(f32[18,8,128]{2,1,0:T(8,128)S(1)} %get-tuple-element.15.all_ref, f32[3,8,128]{2,1,0:T(8,128)S(1)} %get-tuple-element.16.pot_strip_ref, f32[12,8,128]{2,1,0:T(8,128)S(1)} %collective-permute-done.1.recv_ref, ...), custom_call_target="tpu_custom_call" | custom-call | flops 10000000 | bytes 1044480 | tf_op jit(solution)/shard_map/pallas_call | solution.py:578
  17.4 0.1 collective-permute-start.2
  17.5 9.7 %all_to_all.5 = f32[32,1,128]{2,1,0:T(1,128)S(1)} all-to-all(f32[32,1,128]{2,1,0:T(1,128)S(1)} %get-tuple-element.22), channel_id=1, replica_groups=mesh['gx'=2,'gy'=8,'cp'=2] {'gx','gy','cp'}, dimensions={0} | all-to-all | bytes 32768 | tf_op jit(solution)/shard_map/all_to_all | solution.py:677
  27.2 0.0 collective-permute-done.2.other_ref
  27.2 1.6 %shard_map.46 = (f32[8,8,24,128]{3,2,1,0:T(8,128)}, f32[8,8]{1,0:T(8,128)}) custom-call(f32[32,128]{1,0:T(8,128)S(1)} %bitcast.1, f32[8,12,8,128]{3,2,1,0:T(8,128)S(1)} %get-tuple-element.23.own_ref, f32[8,12,8,128]{3,2,1,0:T(8,128)S(1)} %collective-permute-done.2.other_ref), custom_call_target="tpu_custom_call" | custom-call | bytes 1589504 | tf_op jit(solution)/shard_map/pallas_call | solution.py:578
Async XLA Ops:
  0.6 6.6 %copy-start.1 = (f32[8,24,128]{2,1,0:T(8,128)S(1)}, f32[8,24,128]{2,1,0:T(8,128)}, u32[]{:S(2)}) copy-start(f32[8,24,128]{2,1,0:T(8,128)} %pot_ref.3) | copy-start | bytes 294916
  0.6 6.6 %copy-start = (f32[8,8,24,128]{3,2,1,0:T(8,128)S(1)}, f32[8,8,24,128]{3,2,1,0:T(8,128)}, u32[]{:S(2)}) copy-start(f32[8,8,24,128]{3,2,1,0:T(8,128)} %x_ref.1) | copy-start | bytes 2359300
  1.7 10.2 %collective-permute-start = (f32[27,8,128]{2,1,0:T(8,128)S(1)}, f32[27,8,128]{2,1,0:T(8,128)S(1)}, u32[]{:S(2)}, u32[]{:S(2)}) collective-permute-start(f32[27,8,128]{2,1,0:T(8,128)S(1)} %shard_map.41.own_ref), channel_id=1, source_target_pairs={{0,15},{1,2},{2,1},{3,4},{4,3},{5,6},{6,5},{7,8},{8,7},{9,10},{10,... | collective-permute-start | bytes 331784 | tf_op jit(solution)/shard_map/ppermute | solution.py:622
  12.2 4.2 %collective-permute-start.1 = (f32[12,8,128]{2,1,0:T(8,128)S(1)}, f32[12,8,128]{2,1,0:T(8,128)S(1)}, u32[]{:S(2)}, u32[]{:S(2)}) collective-permute-start(f32[12,8,128]{2,1,0:T(8,128)S(1)} %get-tuple-element.17), channel_id=1, source_target_pairs={{0,16},{16,0},{1,17},{17,1},{2,18},{18,2},{3,19},{19,3},{4,20},{20... | collective-permute-start | bytes 147464 | tf_op jit(solution)/shard_map/ppermute | solution.py:646
  17.4 9.8 %collective-permute-start.2 = (f32[8,12,8,128]{3,2,1,0:T(8,128)S(1)}, f32[8,12,8,128]{3,2,1,0:T(8,128)S(1)}, u32[]{:S(2)}, u32[]{:S(2)}) collective-permute-start(f32[8,12,8,128]{3,2,1,0:T(8,128)S(1)} %get-tuple-element.23.own_ref), channel_id=1, source_target_pairs={{0,1},{1,0},{2,3},{3,2},{4,5},{5,4},{6,7},{7,6},{8,9},{9,8},{10,11... | collective-permute-start | bytes 1179656 | tf_op jit(solution)/shard_map/ppermute | solution.py:676

commit v4 on v3

--- a/solution.py
+++ b/solution.py
@@ -119,10 +119,11 @@
 def pack_kernel(x_hbm, pot_hbm, out_ref, window, pot_buf, sems):
     cp = lax.axis_index("cp")
     vectors, nz, rows, _ = x_hbm.shape
-    offset = cp * (rows - SUB)
-    copies = copy_rows(x_hbm, window, sems, SUB, cp)
+    copies = copy_rows(x_hbm, window, sems, SUB, 1 - cp)
     copies.append(
-        pltpu.make_async_copy(pot_hbm.at[:, pl.ds(offset, SUB), :], pot_buf, sems.at[vectors])
+        pltpu.make_async_copy(
+            pot_hbm.at[:, pl.ds((1 - cp) * (rows - SUB), SUB), :], pot_buf, sems.at[vectors]
+        )
     )
     for copy in copies:
         copy.start()
@@ -131,7 +132,7 @@
     flat = window.reshape(nz * vectors * SUB, LANES)
     pot = pot_buf.reshape(nz * SUB, LANES)
     for k in range(REACH):
-        row = k + cp * (SUB - 1 - 2 * k)
+        row = k + (1 - cp) * (SUB - 1 - 2 * k)
         for z in range(nz):
             out_ref[k * nz + z] = flat[pl.ds(z * vectors * SUB + row, vectors, stride=SUB), :]
         out_ref[REACH * nz + k] = pot[pl.ds(row, nz, stride=SUB), :]
@@ -205,7 +206,8 @@
 
 
 def interior_kernel(
-    x_ref, pot_ref, part_ref, edge_ref, strip_ref, pot_strip_ref, window, xs, tab, ub, vb, sems
+    x_ref, pot_ref, part_ref, edge_ref, strip_ref, pot_strip_ref, own_ref,
+    window, xs, tab, ub, vb, sems,
 ):
     cp = lax.axis_index("cp")
     vectors, nz, rows, _ = x_ref.shape
@@ -239,6 +241,10 @@
             xs[1, r, z] = turn(value, 1)
             xs[2, r, z] = turn(value, -1)
             tiles.append(value)
+            if r < REACH - 1:
+                own_ref[r * nz + z] = value
+        if r < REACH - 1:
+            own_ref[(REACH - 1) * nz + r] = tile
         strip_ref[r] = strip_of(tiles)
 
     def x_at(r, d=0):
@@ -333,7 +339,7 @@
         return lambda j, q: [one(j, q, r + d) for d in (-1, 0, 1)]
 
     for r in range(-REACH, 2):
-        tile = own_ref[REACH * nz + r] if r >= 0 else recv_ref[REACH * nz - 1 - r]
+        tile = own_ref[(REACH - 1) * nz + r] if r >= 0 else recv_ref[REACH * nz - 1 - r]
         fill_tables(tab, tile, lambda index: index * span + r + REACH)
     for r in range(-REACH, 2):
         first_step(coefs(r), x_at(r), ub, r + REACH, nz)
@@ -608,22 +614,23 @@
         return pltpu.VMEM(shape + tile, jnp.float32)
 
     count = lax.axis_size("gy")
-    swaps = []
+    rings = []
     for g in range(count):
-        swaps.append((2 * g, 2 * ((g - 1) % count) + 1))
-        swaps.append((2 * g + 1, 2 * ((g + 1) % count)))
-    (own_rows,) = call(
+        rings.append((2 * g, 2 * ((g + 1) % count)))
+        rings.append((2 * g + 1, 2 * ((g - 1) % count) + 1))
+    (rows_out,) = call(
         pack_kernel,
         [pltpu.with_memory_space_constraint(value, hbm) for value in (start_vectors, potential)],
         [(REACH * (nz + 1),) + tile],
         [room(nz, vectors), room(nz), pltpu.SemaphoreType.DMA((vectors + 1,))],
         (hbm, hbm),
     )
-    far_rows = lax.ppermute(own_rows, ("gy", "cp"), swaps)
+    far_rows = lax.ppermute(rows_out, ("gy", "cp"), rings)
     tables = POINTS * TABLES + 1
-    part, edge, strip, pot_strip = call(
+    part, edge, strip, pot_strip, own_rows = call(
         interior_kernel, (start_vectors, potential),
-        [(local - 4, nz) + tile, (POINTS, 2, REACH - 1, nz) + tile, (local,) + tile, (local,) + tile],
+        [(local - 4, nz) + tile, (POINTS, 2, REACH - 1, nz) + tile]
+        + [(local,) + tile] * 2 + [((REACH - 1) * (nz + 1),) + tile],
         [
             pltpu.VMEM((nz, vectors, height, LANES), jnp.float32),
             room(3, local + 2, nz),

time: 28.9 us -> 28.7 us (level)
  starting transfers between devices: 7.17 us -> 5.2 us
  waiting for transfers between devices: 1.35 us -> 2.26 us
  blocking collectives: 9.67 us -> 10.5 us
    ppermute x1, starting transfers between devices: 5.54 us -> 3.05 us  [per_device(): far_rows = lax.ppermute(rows_out, ('gy', 'cp'), rings)]
    ppermute x1, waiting for transfers between devices: 0.01 us -> 1.08 us  [per_device(): far_rows = lax.ppermute(rows_out, ('gy', 'cp'), rings)]
    all_to_all x1, blocking collectives: 9.67 us -> 10.5 us  [per_device(): lax.all_to_all(packet, axes, 0, 0, tiled=True).reshape(devices, LANES)]
    ppermute x1, starting transfers between devices: 0.07 us -> 0.44 us  [per_device(): other = lax.ppermute(own, 'cp', [(0, 1), (1, 0)])]
  transfers between devices with their start and end apart: 3 -> 3, of which waited for: 1 -> 2; matrix products, arithmetic and copies ran while one was open for 0% -> 0% of each run, Pallas kernels for 21% -> 21%
where the time goes in v4:
time: 28.7 us; the launch traced here: 28.6 us
  blocking collectives  10.5 us (37%)
  Pallas kernels  9.87 us (34%)
  starting transfers between devices  5.2 us (18%)
  waiting for transfers between devices  2.26 us (8%)
  between operations  0.69 us (2%)
    all_to_all x1, blocking collectives, per_device(): lax.all_to_all(packet, axes, 0, 0, tiled=True).reshape(devices, LANES)  10.5 us
    pallas_call x6, Pallas kernels, call(): pl.pallas_call(functools.partial(kernel, **options), out_shape=[jax.Shape...  9.87 us
    ppermute x1, starting transfers between devices, per_device(): far_rows = lax.ppermute(rows_out, ('gy', 'cp'), rings)  3.05 us
    ppermute x1, starting transfers between devices, per_device(): recv = lax.ppermute(send, 'gx', ahead)  1.72 us
    ppermute x1, waiting for transfers between devices, per_device(): recv = lax.ppermute(send, 'gx', ahead)  1.18 us
    ppermute x1, waiting for transfers between devices, per_device(): far_rows = lax.ppermute(rows_out, ('gy', 'cp'), rings)  1.08 us
  transfers between devices with their start and end apart: 3, of which 2 were waited for; matrix products, arithmetic and copies ran while one was open for 0% of the time, Pallas kernels for 21%

profile of v4, /device:TPU:0, one launch (start us, length us, event | category | flops | bytes accessed | tf_op | source)
XLA Modules:
  0.0 28.6 jit_solution(13218377967406897547)
XLA Ops:
  0.6 0.0 copy-start.1
  0.6 0.0 copy-start
  0.6 1.1 %shard_map.41 = f32[27,8,128]{2,1,0:T(8,128)S(1)} custom-call(f32[8,8,24,128]{3,2,1,0:T(8,128)} %x_ref.1, f32[8,24,128]{2,1,0:T(8,128)} %pot_ref.3), custom_call_target="tpu_custom_call" | custom-call | bytes 995328 | tf_op jit(solution)/shard_map/pallas_call | solution.py:584
  1.7 3.0 %collective-permute-start = (f32[27,8,128]{2,1,0:T(8,128)S(1)}, f32[27,8,128]{2,1,0:T(8,128)S(1)}, u32[]{:S(2)}, u32[]{:S(2)}) collective-permute-start(f32[27,8,128]{2,1,0:T(8,128)S(1)} %shard_map.41), channel_id=1, source_target_pairs={{0,2},{1,15},{2,4},{3,1},{4,6},{5,3},{6,8},{7,5},{8,10},{9,7},{10,... | collective-permute-start | bytes 331784 | tf_op jit(solution)/shard_map/ppermute | solution.py:628
  4.8 0.0 copy-done.1
  4.8 0.0 copy-done
  4.8 4.7 %shard_map.42 = (f32[11,8,8,128]{3,2,1,0:T(8,128)S(1)}, f32[4,2,2,8,8,128]{5,4,3,2,1,0:T(8,128)S(1)}, f32[15,8,128]{2,1,0:T(8,128)S(1)}, f32[15,8,128]{2,1,0:T(8,128)S(1)}, f32[18,8,128]{2,1,0:T(8,128)S(1)}) custom-call(f32[8,8,24,128]{3,2,1,0:T(8,128)S(1)} %copy-done, f32[8,24,128]{2,1,0:T(8,128)S(1)} %copy-done.1), custom_call_target="tpu_custom_call" | custom-call | flops 100000000 | bytes 1966080 | tf_op jit(solution)/shard_map/pallas_call | solution.py:584
  9.5 1.1 %collective-permute-done.recv_ref = f32[27,8,128]{2,1,0:T(8,128)S(1)} collective-permute-done((f32[27,8,128]{2,1,0:T(8,128)S(1)}, f32[27,8,128]{2,1,0:T(8,128)S(1)}, u32[]{:S(2)}, u32[]{:S(2)}) %collective-permute-start) | collective-permute-done | bytes 110624 | tf_op jit(solution)/shard_map/ppermute | solution.py:628
  10.5 0.2 shard_map.43
  10.8 1.7 %collective-permute-start.1 = (f32[12,8,128]{2,1,0:T(8,128)S(1)}, f32[12,8,128]{2,1,0:T(8,128)S(1)}, u32[]{:S(2)}, u32[]{:S(2)}) collective-permute-start(f32[12,8,128]{2,1,0:T(8,128)S(1)} %get-tuple-element.18), channel_id=1, source_target_pairs={{0,16},{16,0},{1,17},{17,1},{2,18},{18,2},{3,19},{19,3},{4,20},{20... | collective-permute-start | bytes 147464 | tf_op jit(solution)/shard_map/ppermute | solution.py:653
  12.5 1.3 %shard_map.44 = (f32[3,8,8,128]{3,2,1,0:T(8,128)S(1)}, f32[10,8,128]{2,1,0:T(8,128)S(1)}) custom-call(f32[18,8,128]{2,1,0:T(8,128)S(1)} %get-tuple-element.19.own_ref, f32[27,8,128]{2,1,0:T(8,128)S(1)} %collective-permute-done.recv_ref, f32[4,2,2,8,8,128]{5,4,3,2,1,0:T(8,128)S(1)} %get-tuple-element.20.edge_ref, ...), custom_call_target="tpu_custom_call" | custom-call | flops 30000000 | bytes 1306624 | tf_op jit(solution)/shard_map/pallas_call | solution.py:584
  13.8 1.2 %collective-permute-done.1.recv_ref = f32[12,8,128]{2,1,0:T(8,128)S(1)} collective-permute-done((f32[12,8,128]{2,1,0:T(8,128)S(1)}, f32[12,8,128]{2,1,0:T(8,128)S(1)}, u32[]{:S(2)}, u32[]{:S(2)}) %collective-permute-start.1) | collective-permute-done | bytes 49184 | tf_op jit(solution)/shard_map/ppermute | solution.py:653
  15.0 1.0 %shard_map.45 = (f32[8,12,8,128]{3,2,1,0:T(8,128)S(1)}, f32[32,1,128]{2,1,0:T(1,128)S(1)}) custom-call(f32[18,8,128]{2,1,0:T(8,128)S(1)} %get-tuple-element.16.all_ref, f32[3,8,128]{2,1,0:T(8,128)S(1)} %get-tuple-element.17.pot_strip_ref, f32[12,8,128]{2,1,0:T(8,128)S(1)} %collective-permute-done.1.recv_ref, ...), custom_call_target="tpu_custom_call" | custom-call | flops 10000000 | bytes 1044480 | tf_op jit(solution)/shard_map/pallas_call | solution.py:584
  16.0 0.4 %collective-permute-start.2 = (f32[8,12,8,128]{3,2,1,0:T(8,128)S(1)}, f32[8,12,8,128]{3,2,1,0:T(8,128)S(1)}, u32[]{:S(2)}, u32[]{:S(2)}) collective-permute-start(f32[8,12,8,128]{3,2,1,0:T(8,128)S(1)} %get-tuple-element.25.own_ref), channel_id=1, source_target_pairs={{0,1},{1,0},{2,3},{3,2},{4,5},{5,4},{6,7},{7,6},{8,9},{9,8},{10,11... | collective-permute-start | bytes 1179656 | tf_op jit(solution)/shard_map/ppermute | solution.py:683
  16.4 10.5 %all_to_all.5 = f32[32,1,128]{2,1,0:T(1,128)S(1)} all-to-all(f32[32,1,128]{2,1,0:T(1,128)S(1)} %get-tuple-element.24), channel_id=1, replica_groups=mesh['gx'=2,'gy'=8,'cp'=2] {'gx','gy','cp'}, dimensions={0} | all-to-all | bytes 32768 | tf_op jit(solution)/shard_map/all_to_all | solution.py:684
  27.0 0.0 collective-permute-done.2.other_ref
  27.0 1.6 %shard_map.46 = (f32[8,8,24,128]{3,2,1,0:T(8,128)}, f32[8,8]{1,0:T(8,128)}) custom-call(f32[32,128]{1,0:T(8,128)S(1)} %bitcast.1, f32[8,12,8,128]{3,2,1,0:T(8,128)S(1)} %get-tuple-element.25.own_ref, f32[8,12,8,128]{3,2,1,0:T(8,128)S(1)} %collective-permute-done.2.other_ref), custom_call_target="tpu_custom_call" | custom-call | bytes 1589504 | tf_op jit(solution)/shard_map/pallas_call | solution.py:584
Async XLA Ops:
  0.6 4.2 %copy-start.1 = (f32[8,24,128]{2,1,0:T(8,128)S(1)}, f32[8,24,128]{2,1,0:T(8,128)}, u32[]{:S(2)}) copy-start(f32[8,24,128]{2,1,0:T(8,128)} %pot_ref.3) | copy-start | bytes 294916
  0.6 4.1 %copy-start = (f32[8,8,24,128]{3,2,1,0:T(8,128)S(1)}, f32[8,8,24,128]{3,2,1,0:T(8,128)}, u32[]{:S(2)}) copy-start(f32[8,8,24,128]{3,2,1,0:T(8,128)} %x_ref.1) | copy-start | bytes 2359300
  1.7 8.8 %collective-permute-start = (f32[27,8,128]{2,1,0:T(8,128)S(1)}, f32[27,8,128]{2,1,0:T(8,128)S(1)}, u32[]{:S(2)}, u32[]{:S(2)}) collective-permute-start(f32[27,8,128]{2,1,0:T(8,128)S(1)} %shard_map.41), channel_id=1, source_target_pairs={{0,2},{1,15},{2,4},{3,1},{4,6},{5,3},{6,8},{7,5},{8,10},{9,7},{10,... | collective-permute-start | bytes 331784 | tf_op jit(solution)/shard_map/ppermute | solution.py:628
  10.8 4.2 %collective-permute-start.1 = (f32[12,8,128]{2,1,0:T(8,128)S(1)}, f32[12,8,128]{2,1,0:T(8,128)S(1)}, u32[]{:S(2)}, u32[]{:S(2)}) collective-permute-start(f32[12,8,128]{2,1,0:T(8,128)S(1)} %get-tuple-element.18), channel_id=1, source_target_pairs={{0,16},{16,0},{1,17},{17,1},{2,18},{18,2},{3,19},{19,3},{4,20},{20... | collective-permute-start | bytes 147464 | tf_op jit(solution)/shard_map/ppermute | solution.py:653
  16.0 11.0 %collective-permute-start.2 = (f32[8,12,8,128]{3,2,1,0:T(8,128)S(1)}, f32[8,12,8,128]{3,2,1,0:T(8,128)S(1)}, u32[]{:S(2)}, u32[]{:S(2)}) collective-permute-start(f32[8,12,8,128]{3,2,1,0:T(8,128)S(1)} %get-tuple-element.25.own_ref), channel_id=1, source_target_pairs={{0,1},{1,0},{2,3},{3,2},{4,5},{5,4},{6,7},{7,6},{8,9},{9,8},{10,11... | collective-permute-start | bytes 1179656 | tf_op jit(solution)/shard_map/ppermute | solution.py:683

commit v5 on v4

--- a/solution.py
+++ b/solution.py
@@ -142,17 +142,18 @@
     return value if total is None else total + value
 
 
-def fill_tables(tab, tile, slot):
+def fill_tables(tab, tile, slot, steps=3):
     total = None
     sides = (tile, turn(tile, 1), turn(tile, -1))
     for j in range(POINTS):
-        for d, side in enumerate(sides):
+        for d, side in enumerate(sides if steps > 1 else sides[:1]):
             values = coefficients(side, j)
-            for q, value in enumerate(values):
+            for q, value in enumerate(values if steps > 2 else values[:2]):
                 tab[slot(j * TABLES + 4 * d + q)] = value
             if d == 0:
                 total = add(total, values[2])
-    tab[slot(POINTS * TABLES)] = total
+    if steps > 2:
+        tab[slot(POINTS * TABLES)] = total
 
 
 def first_step(coef, x, ub, r, nz):
@@ -231,7 +232,7 @@
 
     for r in range(local):
         tile = pot[pl.ds(r + cp * (rows - 1 - 2 * r), nz, stride=rows), :]
-        fill_tables(tab, tile, lambda index: index * span + r)
+        fill_tables(tab, tile, lambda index: index * span + r, 1 + min(r, local - 1 - r, 2))
         pot_strip_ref[r] = strip_of_layers(tile)
         tiles = []
         for z in range(nz):
@@ -340,7 +341,7 @@
 
     for r in range(-REACH, 2):
         tile = own_ref[(REACH - 1) * nz + r] if r >= 0 else recv_ref[REACH * nz - 1 - r]
-        fill_tables(tab, tile, lambda index: index * span + r + REACH)
+        fill_tables(tab, tile, lambda index: index * span + r + REACH, min(r + REACH, 2) + 1)
     for r in range(-REACH, 2):
         first_step(coefs(r), x_at(r), ub, r + REACH, nz)
     for r in range(1 - REACH, 1):

time: 28.7 us -> 28.7 us (level)
  no operation moved by 1% of the time
where the time goes in v5:
time: 28.7 us; the launch traced here: 28.6 us
  blocking collectives  10.5 us (37%)
  Pallas kernels  9.86 us (34%)
  starting transfers between devices  5.2 us (18%)
  waiting for transfers between devices  2.28 us (8%)
  between operations  0.69 us (2%)
    all_to_all x1, blocking collectives, per_device(): lax.all_to_all(packet, axes, 0, 0, tiled=True).reshape(devices, LANES)  10.5 us
    pallas_call x6, Pallas kernels, call(): pl.pallas_call(functools.partial(kernel, **options), out_shape=[jax.Shape...  9.86 us
    ppermute x1, starting transfers between devices, per_device(): far_rows = lax.ppermute(rows_out, ('gy', 'cp'), rings)  3.05 us
    ppermute x1, starting transfers between devices, per_device(): recv = lax.ppermute(send, 'gx', ahead)  1.72 us
    ppermute x1, waiting for transfers between devices, per_device(): recv = lax.ppermute(send, 'gx', ahead)  1.19 us
    ppermute x1, waiting for transfers between devices, per_device(): far_rows = lax.ppermute(rows_out, ('gy', 'cp'), rings)  1.09 us
  transfers between devices with their start and end apart: 3, of which 2 were waited for; matrix products, arithmetic and copies ran while one was open for 0% of the time, Pallas kernels for 21%

profile of v5, /device:TPU:0, one launch (start us, length us, event | category | flops | bytes accessed | tf_op | source)
XLA Modules:
  0.0 28.6 jit_solution(10338984257325355854)
XLA Ops:
  0.6 0.0 copy-start.1
  0.6 0.0 copy-start
  0.6 1.1 %shard_map.41 = f32[27,8,128]{2,1,0:T(8,128)S(1)} custom-call(f32[8,8,24,128]{3,2,1,0:T(8,128)} %x_ref.1, f32[8,24,128]{2,1,0:T(8,128)} %pot_ref.3), custom_call_target="tpu_custom_call" | custom-call | bytes 995328 | tf_op jit(solution)/shard_map/pallas_call | solution.py:585
  1.7 3.0 %collective-permute-start = (f32[27,8,128]{2,1,0:T(8,128)S(1)}, f32[27,8,128]{2,1,0:T(8,128)S(1)}, u32[]{:S(2)}, u32[]{:S(2)}) collective-permute-start(f32[27,8,128]{2,1,0:T(8,128)S(1)} %shard_map.41), channel_id=1, source_target_pairs={{0,2},{1,15},{2,4},{3,1},{4,6},{5,3},{6,8},{7,5},{8,10},{9,7},{10,... | collective-permute-start | bytes 331784 | tf_op jit(solution)/shard_map/ppermute | solution.py:629
  4.8 0.0 copy-done.1
  4.8 0.0 copy-done
  4.8 4.7 %shard_map.42 = (f32[11,8,8,128]{3,2,1,0:T(8,128)S(1)}, f32[4,2,2,8,8,128]{5,4,3,2,1,0:T(8,128)S(1)}, f32[15,8,128]{2,1,0:T(8,128)S(1)}, f32[15,8,128]{2,1,0:T(8,128)S(1)}, f32[18,8,128]{2,1,0:T(8,128)S(1)}) custom-call(f32[8,8,24,128]{3,2,1,0:T(8,128)S(1)} %copy-done, f32[8,24,128]{2,1,0:T(8,128)S(1)} %copy-done.1), custom_call_target="tpu_custom_call" | custom-call | flops 100000000 | bytes 1966080 | tf_op jit(solution)/shard_map/pallas_call | solution.py:585
  9.5 1.1 %collective-permute-done.recv_ref = f32[27,8,128]{2,1,0:T(8,128)S(1)} collective-permute-done((f32[27,8,128]{2,1,0:T(8,128)S(1)}, f32[27,8,128]{2,1,0:T(8,128)S(1)}, u32[]{:S(2)}, u32[]{:S(2)}) %collective-permute-start) | collective-permute-done | bytes 110624 | tf_op jit(solution)/shard_map/ppermute | solution.py:629
  10.5 0.2 shard_map.43
  10.8 1.7 %collective-permute-start.1 = (f32[12,8,128]{2,1,0:T(8,128)S(1)}, f32[12,8,128]{2,1,0:T(8,128)S(1)}, u32[]{:S(2)}, u32[]{:S(2)}) collective-permute-start(f32[12,8,128]{2,1,0:T(8,128)S(1)} %get-tuple-element.18), channel_id=1, source_target_pairs={{0,16},{16,0},{1,17},{17,1},{2,18},{18,2},{3,19},{19,3},{4,20},{20... | collective-permute-start | bytes 147464 | tf_op jit(solution)/shard_map/ppermute | solution.py:654
  12.5 1.2 %shard_map.44 = (f32[3,8,8,128]{3,2,1,0:T(8,128)S(1)}, f32[10,8,128]{2,1,0:T(8,128)S(1)}) custom-call(f32[18,8,128]{2,1,0:T(8,128)S(1)} %get-tuple-element.19.own_ref, f32[27,8,128]{2,1,0:T(8,128)S(1)} %collective-permute-done.recv_ref, f32[4,2,2,8,8,128]{5,4,3,2,1,0:T(8,128)S(1)} %get-tuple-element.20.edge_ref, ...), custom_call_target="tpu_custom_call" | custom-call | flops 30000000 | bytes 1306624 | tf_op jit(solution)/shard_map/pallas_call | solution.py:585
  13.8 1.2 %collective-permute-done.1.recv_ref = f32[12,8,128]{2,1,0:T(8,128)S(1)} collective-permute-done((f32[12,8,128]{2,1,0:T(8,128)S(1)}, f32[12,8,128]{2,1,0:T(8,128)S(1)}, u32[]{:S(2)}, u32[]{:S(2)}) %collective-permute-start.1) | collective-permute-done | bytes 49184 | tf_op jit(solution)/shard_map/ppermute | solution.py:654
  15.0 1.0 %shard_map.45 = (f32[8,12,8,128]{3,2,1,0:T(8,128)S(1)}, f32[32,1,128]{2,1,0:T(1,128)S(1)}) custom-call(f32[18,8,128]{2,1,0:T(8,128)S(1)} %get-tuple-element.16.all_ref, f32[3,8,128]{2,1,0:T(8,128)S(1)} %get-tuple-element.17.pot_strip_ref, f32[12,8,128]{2,1,0:T(8,128)S(1)} %collective-permute-done.1.recv_ref, ...), custom_call_target="tpu_custom_call" | custom-call | flops 10000000 | bytes 1044480 | tf_op jit(solution)/shard_map/pallas_call | solution.py:585
  16.0 0.4 %collective-permute-start.2 = (f32[8,12,8,128]{3,2,1,0:T(8,128)S(1)}, f32[8,12,8,128]{3,2,1,0:T(8,128)S(1)}, u32[]{:S(2)}, u32[]{:S(2)}) collective-permute-start(f32[8,12,8,128]{3,2,1,0:T(8,128)S(1)} %get-tuple-element.25.own_ref), channel_id=1, source_target_pairs={{0,1},{1,0},{2,3},{3,2},{4,5},{5,4},{6,7},{7,6},{8,9},{9,8},{10,11... | collective-permute-start | bytes 1179656 | tf_op jit(solution)/shard_map/ppermute | solution.py:684
  16.4 10.5 %all_to_all.5 = f32[32,1,128]{2,1,0:T(1,128)S(1)} all-to-all(f32[32,1,128]{2,1,0:T(1,128)S(1)} %get-tuple-element.24), channel_id=1, replica_groups=mesh['gx'=2,'gy'=8,'cp'=2] {'gx','gy','cp'}, dimensions={0} | all-to-all | bytes 32768 | tf_op jit(solution)/shard_map/all_to_all | solution.py:685
  27.0 0.0 collective-permute-done.2.other_ref
  27.0 1.6 %shard_map.46 = (f32[8,8,24,128]{3,2,1,0:T(8,128)}, f32[8,8]{1,0:T(8,128)}) custom-call(f32[32,128]{1,0:T(8,128)S(1)} %bitcast.1, f32[8,12,8,128]{3,2,1,0:T(8,128)S(1)} %get-tuple-element.25.own_ref, f32[8,12,8,128]{3,2,1,0:T(8,128)S(1)} %collective-permute-done.2.other_ref), custom_call_target="tpu_custom_call" | custom-call | bytes 1589504 | tf_op jit(solution)/shard_map/pallas_call | solution.py:585
Async XLA Ops:
  0.6 4.2 %copy-start.1 = (f32[8,24,128]{2,1,0:T(8,128)S(1)}, f32[8,24,128]{2,1,0:T(8,128)}, u32[]{:S(2)}) copy-start(f32[8,24,128]{2,1,0:T(8,128)} %pot_ref.3) | copy-start | bytes 294916
  0.6 4.1 %copy-start = (f32[8,8,24,128]{3,2,1,0:T(8,128)S(1)}, f32[8,8,24,128]{3,2,1,0:T(8,128)}, u32[]{:S(2)}) copy-start(f32[8,8,24,128]{3,2,1,0:T(8,128)} %x_ref.1) | copy-start | bytes 2359300
  1.7 8.8 %collective-permute-start = (f32[27,8,128]{2,1,0:T(8,128)S(1)}, f32[27,8,128]{2,1,0:T(8,128)S(1)}, u32[]{:S(2)}, u32[]{:S(2)}) collective-permute-start(f32[27,8,128]{2,1,0:T(8,128)S(1)} %shard_map.41), channel_id=1, source_target_pairs={{0,2},{1,15},{2,4},{3,1},{4,6},{5,3},{6,8},{7,5},{8,10},{9,7},{10,... | collective-permute-start | bytes 331784 | tf_op jit(solution)/shard_map/ppermute | solution.py:629
  10.8 4.2 %collective-permute-start.1 = (f32[12,8,128]{2,1,0:T(8,128)S(1)}, f32[12,8,128]{2,1,0:T(8,128)S(1)}, u32[]{:S(2)}, u32[]{:S(2)}) collective-permute-start(f32[12,8,128]{2,1,0:T(8,128)S(1)} %get-tuple-element.18), channel_id=1, source_target_pairs={{0,16},{16,0},{1,17},{17,1},{2,18},{18,2},{3,19},{19,3},{4,20},{20... | collective-permute-start | bytes 147464 | tf_op jit(solution)/shard_map/ppermute | solution.py:654
  16.0 11.0 %collective-permute-start.2 = (f32[8,12,8,128]{3,2,1,0:T(8,128)S(1)}, f32[8,12,8,128]{3,2,1,0:T(8,128)S(1)}, u32[]{:S(2)}, u32[]{:S(2)}) collective-permute-start(f32[8,12,8,128]{3,2,1,0:T(8,128)S(1)} %get-tuple-element.25.own_ref), channel_id=1, source_target_pairs={{0,1},{1,0},{2,3},{3,2},{4,5},{5,4},{6,7},{7,6},{8,9},{9,8},{10,11... | collective-permute-start | bytes 1179656 | tf_op jit(solution)/shard_map/ppermute | solution.py:684
